TPU v7x, 128 devices: a whole 4x4x4 slice. The times are simulated.
128 devices in a mesh: ctx: 16 (over x_hi, y, core), tp: 8 (over z, x_lo).
Axes of the slice: x: 4 (x_hi: 2, x_lo: 2; x = x_hi * 2 + x_lo), y: 4, z: 4, core: 2. Of those that a mesh axis runs over, the one named last changes fastest.
Arguments:
- residual_in: bfloat16 [2, 4096, 4096], P(None, 'ctx', 'tp'), may hold values from -6 to 6
- mr_qkv: bfloat16 [2, 4096, 3, 4096], P(None, 'ctx', None, 'tp'), may hold values from -6 to 6
- mr_short_w: float32 [3, 3, 4096], P(None, None, 'tp'), may hold values from -3.5 to 3.5
- mr_filter: bfloat16 [128, 4096], P(None, 'tp'), may hold values from -0.5 to 0.5
- mr_skip: float32 [4096], P('tp'), may hold values from -4 to 4
- mr_out_w: bfloat16 [4096, 4096], P('tp', 'ctx'), may hold values from -0.09375 to 0.09375
- lr_gain: float32 [4096], replicated, may hold values from 0.1 to 1.9
- lr_in_w: bfloat16 [4096, 3, 4096], P(None, None, 'tp'), may hold values from -0.09375 to 0.09375
- lr_short_w: float32 [3, 3, 4096], P(None, None, 'tp'), may hold values from -3.5 to 3.5
- lr_rate: float32 [16, 4096], P(None, 'tp'), may hold values from 0 to 1, as said below
- lr_res: float32 [16, 4096], P(None, 'tp'), may hold values from -3 to 3
- lr_skip: float32 [4096], P('tp'), may hold values from -4 to 4
- lr_out_w: bfloat16 [4096, 4096], P('tp', 'ctx'), may hold values from -0.09375 to 0.09375
Outputs:
- residual_out: bfloat16 [2, 4096, 4096], P(None, 'ctx', 'tp')
Inputs may be any that keep to these rules, and one draw needn't show every extreme that they name: `lr_rate`: each rate lies between 0.1 / 4096 and 1 / 20.
All inputs are finite; a program needn't handle non-finite values.
Results may differ from a plain program's by a relative error of at most 0.034.
Values may be sent and summed in bfloat16 or wider, within the bound.
A program may use at most 192 MiB of HBM per device.

v0:
```python
import jax
import jax.numpy as jnp
from jax import lax
from jax.experimental import pallas as pl
from jax.experimental.pallas import tpu as pltpu
from jax.sharding import PartitionSpec as P

MESH = pl.DeviceIdType.MESH
F32 = jnp.float32
BF16 = jnp.bfloat16

SEGS = 8
STEPS = 64
ROWS = SEGS * STEPS
WIDTH = 512
TAPS = 128
POLES = 16
LANES = 128


def kernel(
    res_h, qkv_h, sw1, filt, skip1, wo1_h, gain, win_h, sw2, rate, resid, skip2, wo2_h,
    out_h,
    qkv_v, xtail, x32, q32, uext, fb, pk_s, pk_r, zo, zn, w, win, ps, pr, pacc, mid, scaled, acc, ssq,
    ltail_s, ltail, est, st_s, st_r, hin, obf, resv,
    loc, hs, hr, wsnd, fsnd, wrecv, zs, zr, pss, prs, ags, agr, sts, strv,
):
    c = lax.axis_index("ctx")
    t = lax.axis_index("tp")
    core = c % 2
    m = c // 2
    y = m % 4
    z = t // 2
    xl = t % 2
    sib = c + 1 - 2 * core
    xn = t + 1 - 2 * xl

    def ztp(dz, x):
        return ((z + dz) % 4) * 2 + x

    def remote(src, dst, ssem, rsem, ctx, tp):
        return pltpu.make_async_remote_copy(
            src_ref=src,
            dst_ref=dst,
            send_sem=ssem,
            recv_sem=rsem,
            device_id={"ctx": ctx, "tp": tp},
            device_id_type=MESH,
        )

    def arrived(ref, sem):
        pltpu.make_async_copy(ref, ref, sem).wait()

    load_qkv = pltpu.make_async_copy(qkv_h, qkv_v, loc.at[0])
    load_qkv.start()
    load_res = pltpu.make_async_copy(res_h, resv, loc.at[1])
    load_res.start()

    barrier = pltpu.get_barrier_semaphore()

    def greet(ctx, tp):
        pl.semaphore_signal(barrier, inc=1, device_id={"ctx": ctx, "tp": tp}, device_id_type=MESH)

    for d in range(1, 16):
        greet((c + d) % 16, t)
    greet(c, xn)
    for d in range(1, 4):
        greet(c, ztp(d, xl))
    for q in range(4):
        greet(2 * (2 * q + xl) + core, xn)
    pl.semaphore_wait(barrier, 19 + 8 * ((y + xl) % 2))

    tail_copy = remote(qkv_h.at[:, :, 248:256, :], xtail, hs.at[0], hr.at[0], (c + 1) % 16, t)
    tail_copy.start()

    slot_mine = xl * 4 + m // 2
    same = (y + xl) % 2 == 0

    def weight_copies(stage, source):
        home = pltpu.make_async_copy(source, w.at[stage, slot_mine, core], wrecv.at[stage, slot_mine, core])
        far = [
            remote(
                source,
                w.at[stage, slot_mine, core],
                wsnd.at[stage, d],
                wrecv.at[stage, slot_mine, core],
                2 * ((m + d) % 8) + core,
                2 * z + y % 2,
            )
            for d in range(8)
        ]
        return home, far

    def weight_start(stage, source):
        home, far = weight_copies(stage, source)
        for d in (4, 2, 6, 1, 3, 5, 7):
            far[d].start()

        @pl.when(same)
        def _():
            home.start()

        @pl.when(jnp.logical_not(same))
        def _():
            far[0].start()

    def weight_forward(stage, index):
        arrived(w.at[stage, index, core], wrecv.at[stage, index, core])
        remote(
            w.at[stage, index, core],
            w.at[stage, index, core],
            fsnd.at[stage, index],
            wrecv.at[stage, index, core],
            sib,
            t,
        ).start()

    def weight_sibling(stage, index):
        arrived(w.at[stage, index, 1 - core], wrecv.at[stage, index, 1 - core])

    def weight_drain(stage, source):
        _, far = weight_copies(stage, source)
        for d in range(1, 8):
            far[d].wait_send()

        @pl.when(jnp.logical_not(same))
        def _():
            far[0].wait_send()

        for index in range(8):
            remote(
                w.at[stage, index, core],
                w.at[stage, index, core],
                fsnd.at[stage, index],
                wrecv.at[stage, index, core],
                sib,
                t,
            ).wait_send()

    weight_start(0, wo1_h)
    load_win = pltpu.make_async_copy(win_h, win, loc.at[2])

    seg = lax.broadcasted_iota(jnp.int32, (SEGS, WIDTH), 0)
    seg1 = lax.broadcasted_iota(jnp.int32, (SEGS, LANES), 0)
    first = seg % 4 == 0
    live = jnp.where(c > 0, 1.0, 0.0).astype(F32)

    def rows(j, count=1):
        start = j * SEGS
        return pl.ds(start if isinstance(start, int) else pl.multiple_of(start, SEGS), count * SEGS)

    def lanes(lt):
        return pl.ds(pl.multiple_of(lt * LANES, LANES), LANES)

    @pl.loop(0, TAPS // 8)
    def _(i):
        taps = filt[pl.ds(pl.multiple_of(i * 8, 8), 8), :].astype(F32)
        for k in range(8):
            fb[rows(i * 8 + k), :] = jnp.broadcast_to(taps[k : k + 1, :], (SEGS, WIDTH))

    load_qkv.wait()
    for s in range(2):
        for p in range(3):

            @pl.loop(0, 16)
            def _(i, s=s, p=p):
                here = pl.ds(pl.multiple_of(i * 16, 16), 16)
                there = pl.ds(pl.multiple_of(s * 256 + i * 16, 16), 16)
                values = qkv_v[s, p, here, :].astype(F32)
                for k in range(WIDTH // LANES):
                    x32[p, k, there, :] = values[:, LANES * k : LANES * (k + 1)]

    def tap(ref, lag, p):
        return jnp.broadcast_to(ref[3 * lag + p : 3 * lag + p + 1, :], (SEGS, WIDTH))

    def strided3(p, j):
        return jnp.concatenate(
            [x32[p, k, pl.ds(j, SEGS, stride=STEPS), :] for k in range(WIDTH // LANES)], axis=1
        )

    def medium(j, now, before, before2):
        mixed = [tap(sw1, 0, p) * now[p] + tap(sw1, 1, p) * before[p] + tap(sw1, 2, p) * before2[p] for p in range(3)]
        q32[rows(j), :] = mixed[0]
        uext[rows(j + 128), :] = (mixed[1] * mixed[2]).astype(BF16).astype(F32)

    last = [strided3(p, 63) for p in range(3)]
    last2 = [strided3(p, 62) for p in range(3)]
    x0 = [strided3(p, 0) for p in range(3)]
    x1 = [strided3(p, 1) for p in range(3)]
    own1 = [jnp.where(first, 0.0, pltpu.roll(v, 1, 0)) for v in last]
    own2 = [jnp.where(first, 0.0, pltpu.roll(v, 1, 0)) for v in last2]
    medium(0, x0, own1, own2)
    medium(1, x1, x0, own1)

    @pl.loop(2, STEPS)
    def _(j):
        medium(
            j,
            [strided3(p, j) for p in range(3)],
            [strided3(p, j - 1) for p in range(3)],
            [strided3(p, j - 2) for p in range(3)],
        )

    @pl.loop(0, STEPS // 4)
    def _(i):
        packed = []
        for k in range(2):
            even = uext[rows(128 + 4 * i + 2 * k), :]
            odd = uext[rows(129 + 4 * i + 2 * k), :]
            packed.append(jnp.where(seg % 4 >= 2, even, pltpu.roll(odd, 6, 0)))
        pk_s[pl.ds(pl.multiple_of(i * 16, 16), 16), :] = jnp.concatenate(packed, axis=0).astype(BF16)

    u_copy = remote(pk_s, pk_r, hs.at[1], hr.at[1], (c + 1) % 16, t)
    u_copy.start()

    arrived(xtail, hr.at[0])

    def halo(p, row):
        top = xtail[0, p].astype(F32)[row : row + 1, :] * live
        bottom = xtail[1, p].astype(F32)[row : row + 1, :] * live
        return jnp.where(seg < 4, jnp.broadcast_to(top, (SEGS, WIDTH)), jnp.broadcast_to(bottom, (SEGS, WIDTH)))

    full1 = [jnp.where(first, halo(p, 7), own1[p]) for p in range(3)]
    full2 = [jnp.where(first, halo(p, 6), own2[p]) for p in range(3)]
    medium(0, x0, full1, full2)
    medium(1, x1, x0, full1)

    load_win.start()
    arrived(pk_r, hr.at[1])

    @pl.loop(0, STEPS // 2)
    def _(i):
        both = pk_r[pl.ds(pl.multiple_of((i // 2) * 16, 16), 16), :].astype(F32) * live
        got = jnp.where(i % 2 == 0, both[:SEGS], both[SEGS:])
        even = uext[rows(128 + 2 * i), :]
        odd = uext[rows(129 + 2 * i), :]
        uext[rows(64 + 2 * i), :] = jnp.where(first, pltpu.roll(got, 5, 0), pltpu.roll(even, 1, 0))
        uext[rows(65 + 2 * i), :] = jnp.where(first, pltpu.roll(got, 7, 0), pltpu.roll(odd, 1, 0))
        uext[rows(2 * i), :] = jnp.where(seg % 4 < 2, pltpu.roll(got, 6, 0), pltpu.roll(even, 2, 0))
        uext[rows(1 + 2 * i), :] = jnp.where(seg % 4 < 2, got, pltpu.roll(odd, 2, 0))

    def z_copy(stage, kh):
        return remote(zo.at[stage, kh], zn.at[stage, kh], zs.at[stage, kh], zr.at[stage, kh], c, xn)

    def p_copy(stage, d):
        return remote(
            ps.at[stage, d - 1], pr.at[stage, d - 1], pss.at[stage, d - 1], prs.at[stage, d - 1], c, ztp(d, xl)
        )

    def project(stage):
        for kh in range(2):
            arrived(zn.at[stage, kh], zr.at[stage, kh])
        for d in (2, 1, 3, 0):
            dest = (z + d) % 4
            for source in range(2):
                weight_sibling(stage, source * 4 + dest)

            @pl.loop(0, 2)
            def _(half, d=d, dest=dest):
                mine = xl * 4 + dest
                other = (1 - xl) * 4 + dest
                total = jnp.zeros((ROWS, 256), F32)
                for kh in range(2):
                    ks = pl.ds(256 * kh, 256)
                    total += jnp.dot(zo[stage, kh], w[stage, mine, half, ks, :], preferred_element_type=F32)
                    total += jnp.dot(zn[stage, kh], w[stage, other, half, ks, :], preferred_element_type=F32)
                cols = pl.ds(pl.multiple_of(half * 256, 256), 256)
                if d == 0:
                    pacc[:, cols] = total
                else:
                    ps[stage, d - 1, :, cols] = total.astype(BF16)

            if d:
                p_copy(stage, d).start()
        for d in (1, 3, 2):
            arrived(pr.at[stage, d - 1], prs.at[stage, d - 1])

    def project_drain(stage):
        for kh in range(2):
            z_copy(stage, kh).wait_send()
        for d in range(1, 4):
            p_copy(stage, d).wait_send()

    def arrivals(stage, i):
        here = pl.ds(pl.multiple_of(i * 16, 16), 16)
        total = pacc[here, :]
        for k in range(3):
            total += pr[stage, k, here, :].astype(F32)
        return total

    for kh in range(2):

        @pl.loop(0, 8)
        def _(block, kh=kh):
            lane = lanes(kh * 2 + block // 4)
            j0 = (block % 4) * 16

            def taps8(ib, totals):
                base = 128 + j0 - 8 * ib - 7
                window = uext[pl.ds(pl.multiple_of(base * SEGS, SEGS), 23 * SEGS), lane]
                weights = fb[pl.ds(pl.multiple_of(ib * 64, 64), 64), lane]
                totals = list(totals)
                for b in range(8):
                    f = weights[b * SEGS : (b + 1) * SEGS]
                    for a in range(16):
                        k = a + 7 - b
                        totals[a] = totals[a] + f * window[k * SEGS : (k + 1) * SEGS]
                return tuple(totals)

            totals = lax.fori_loop(0, 16, taps8, tuple(jnp.zeros((SEGS, LANES), F32) for _ in range(16)))
            skip = jnp.broadcast_to(skip1[:, lane], (SEGS, LANES))
            out_lane = lanes(block // 4)
            for a in range(0, 16, 2):
                pair = []
                for k in (a, a + 1):
                    u = uext[rows(128 + j0 + k), lane]
                    pair.append(q32[rows(j0 + k), lane] * (totals[k] + skip * u))
                zo[0, kh, pl.ds(pl.multiple_of((j0 + a) * SEGS, 16), 16), out_lane] = jnp.concatenate(
                    pair, axis=0
                ).astype(BF16)

        z_copy(0, kh).start()

    for d in (2, 1, 3, 0):
        for source in range(2):
            weight_forward(0, source * 4 + (z + d) % 4)
    project(0)
    weight_start(1, wo2_h)

    load_res.wait()

    @pl.loop(0, 32)
    def _(i):
        s = i // 16
        r = (i % 16) * 16
        values = resv[s, pl.ds(pl.multiple_of(r, 16), 16), :].astype(F32)
        for k in range(WIDTH // LANES):
            x32[0, k, pl.ds(pl.multiple_of(i * 16, 16), 16), :] = values[:, LANES * k : LANES * (k + 1)]

    @pl.loop(0, 32)
    def _(i):
        before = jnp.concatenate([strided3(0, 2 * i), strided3(0, 2 * i + 1)], axis=0)
        value = (before + arrivals(0, i)).astype(BF16)
        mid[t, i // 8, pl.ds(pl.multiple_of((i % 8) * 16, 16), 16), :] = value

    sent = []

    def send(slot, quarter, tp):
        k = len(sent)
        copy = remote(
            mid.at[slot, quarter], mid.at[slot, quarter], ags.at[k], agr.at[slot, quarter], c, tp
        )
        copy.start()
        sent.append(copy)

    def have(slot, *quarters):
        for quarter in quarters:
            arrived(mid.at[slot, quarter], agr.at[slot, quarter])

    load_win.wait()

    def absorb(slot, fresh=False):
        scale = gain[pl.ds(slot, 1), :]

        @pl.loop(0, 16)
        def _(i):
            here = pl.ds(pl.multiple_of((i % 4) * 32, 32), 32)
            values = mid[slot, i // 4, here, :].astype(F32)
            square = values * values
            part = square[:, 0:128] + square[:, 128:256] + square[:, 256:384] + square[:, 384:512]
            there = pl.ds(pl.multiple_of(i * 32, 32), 32)
            ssq[there, :] = part if fresh else ssq[there, :] + part
            scaled[there, :] = (values * scale).astype(BF16)

        @pl.loop(0, 6)
        def _(i):
            cols = pl.ds(pl.multiple_of((i % 2) * 256, 256), 256)
            depth = pl.ds(pl.multiple_of(slot * WIDTH, WIDTH), WIDTH)
            product = jnp.dot(scaled[...], win[i // 2, depth, cols], preferred_element_type=F32)
            acc[i // 2, :, cols] = product if fresh else acc[i // 2, :, cols] + product

    zp, zm, zz = ztp(1, xl), ztp(3, xl), ztp(2, xl)
    xp, xm, xz = ztp(1, 1 - xl), ztp(3, 1 - xl), ztp(2, 1 - xl)
    for quarter in range(4):
        send(t, quarter, xn)
        send(t, quarter, zp)
        send(t, quarter, zm)
    absorb(t, fresh=True)
    have(xn, 0, 1)
    for quarter in range(2):
        send(xn, quarter, zp)
        send(xn, quarter, zm)
    have(zm, 0, 1, 2, 3)
    send(zm, 0, zp)
    send(zm, 2, zp)
    send(zm, 2, xn)
    send(zm, 3, xn)
    have(zp, 0, 1, 2, 3)
    send(zp, 1, zm)
    send(zp, 3, zm)
    send(zp, 2, xn)
    send(zp, 3, xn)
    absorb(zm)
    absorb(zp)
    have(xm, 0, 1)
    send(xm, 0, zp)
    have(xp, 0, 1)
    send(xp, 1, zm)
    have(zz, 0, 1, 2, 3)
    send(zz, 2, xn)
    send(zz, 3, xn)
    have(xn, 2, 3)
    absorb(xn)
    absorb(zz)
    have(xm, 2, 3)
    absorb(xm)
    have(xp, 2, 3)
    absorb(xp)
    have(xz, 0, 1, 2, 3)
    absorb(xz)

    for d in (2, 1, 3, 0):
        for source in range(2):
            weight_forward(1, source * 4 + (z + d) % 4)

    def finish(i):
        here = pl.ds(i * 16 if isinstance(i, int) else pl.multiple_of(i * 16, 16), 16)
        meansq = jnp.sum(ssq[here, :], axis=1, keepdims=True) * (1.0 / 4096.0)
        factor = lax.rsqrt(meansq + 1e-6)
        values = [(acc[p, here, :] * factor).astype(BF16) for p in range(3)]
        for p in range(3):
            acc[p, here, :] = values[p].astype(F32)
        return values

    tails = finish(31)
    for p in range(3):
        ltail_s[p] = tails[p]
    l_copy = remote(ltail_s, ltail, hs.at[2], hr.at[2], (c + 1) % 16, t)
    l_copy.start()

    @pl.loop(0, 31)
    def _(i):
        finish(i)

    def longer(j, now, before, before2):
        mixed = [tap(sw2, 0, p) * now[p] + tap(sw2, 1, p) * before[p] + tap(sw2, 2, p) * before2[p] for p in range(3)]
        q32[rows(j), :] = mixed[0]
        uext[rows(j), :] = mixed[1] * mixed[2]

    @pl.loop(2, STEPS)
    def _(j):
        longer(
            j,
            [acc[p, rows(j), :] for p in range(3)],
            [acc[p, rows(j - 1), :] for p in range(3)],
            [acc[p, rows(j - 2), :] for p in range(3)],
        )

    arrived(ltail, hr.at[2])
    edge1, edge2 = [], []
    for p in range(3):
        got = ltail[p].astype(F32) * live
        edge2.append(jnp.where(first, pltpu.roll(got[:SEGS], 5, 0), pltpu.roll(acc[p, rows(62), :], 1, 0)))
        edge1.append(jnp.where(first, pltpu.roll(got[SEGS:], 5, 0), pltpu.roll(acc[p, rows(63), :], 1, 0)))
    y0 = [acc[p, rows(0), :] for p in range(3)]
    y1 = [acc[p, rows(1), :] for p in range(3)]
    longer(0, y0, edge1, edge2)
    longer(1, y1, y0, edge1)

    def row_of(ref, n, lane):
        return jnp.broadcast_to(ref[n : n + 1, lane], (SEGS, LANES))

    @pl.loop(0, WIDTH // LANES)
    def _(lt):
        lane = lanes(lt)
        decay = [jnp.exp(-row_of(rate, n, lane)) for n in range(POLES)]

        def step(j, states):
            u = uext[rows(j), lane]
            return tuple(decay[n] * states[n] + u for n in range(POLES))

        states = lax.fori_loop(0, STEPS, step, tuple(jnp.zeros((SEGS, LANES), F32) for _ in range(POLES)))
        for n in range(POLES):
            est[rows(n), lane] = states[n]

    place = seg1 % 4

    @pl.loop(0, WIDTH // LANES)
    def _(lt):
        lane = lanes(lt)
        for g in range(2):
            packed = []
            for h in range(2):
                total = jnp.zeros((SEGS, LANES), F32)
                for r in range(4):
                    n = g * 8 + h * 4 + r
                    span = jnp.exp(-float(STEPS) * row_of(rate, n, lane))
                    value = est[rows(n), lane]
                    value = value + span * jnp.where(place >= 1, pltpu.roll(value, 1, 0), 0.0)
                    value = value + span * span * jnp.where(place >= 2, pltpu.roll(value, 2, 0), 0.0)
                    est[rows(n), lane] = jnp.where(place >= 1, pltpu.roll(value, 1, 0), 0.0)
                    end = value if r == 3 else pltpu.roll(value, (r - 3) % 8, 0)
                    total = jnp.where(place == r, end, total)
                packed.append(total)
            st_s[pl.ds(g * 16, 16), lane] = jnp.concatenate(packed, axis=0).astype(BF16)

    def state_copy(d):
        return remote(st_s, st_r.at[d - 1], sts.at[d - 1], strv.at[d - 1], c + d, t)

    for d in range(15, 0, -1):

        @pl.when(c + d < 16)
        def _(d=d):
            state_copy(d).start()

    packs = []
    for g in range(4):
        total = jnp.zeros((SEGS, WIDTH), F32)
        for r in range(4):
            n = g * 4 + r
            total = jnp.where(seg % 4 == r, jnp.broadcast_to(rate[n : n + 1, :], (SEGS, WIDTH)), total)
        packs.append(total)
    pack = jnp.concatenate(packs, axis=0)
    hin[...] = jnp.zeros((4 * SEGS, WIDTH), F32)
    for d in range(1, 16):

        @pl.when(c - d >= 0)
        def _(d=d):
            arrived(st_r.at[d - 1], strv.at[d - 1])
            hin[...] += jnp.exp(pack * (-256.0 * (d - 1))) * st_r[d - 1].astype(F32)

    for kh in range(2):

        @pl.loop(0, 2)
        def _(half, kh=kh):
            lane = lanes(kh * 2 + half)
            decay, weight, states = [], [], []
            for n in range(POLES):
                r = row_of(rate, n, lane)
                decay.append(jnp.exp(-r))
                weight.append(row_of(resid, n, lane) * jnp.sqrt(1.0 - jnp.exp(-2.0 * r)))
                k = (n // 4) * SEGS + n % 4
                enter = jnp.where(
                    seg1 < 4,
                    jnp.broadcast_to(hin[k : k + 1, lane], (SEGS, LANES)),
                    jnp.broadcast_to(hin[k + 4 : k + 5, lane], (SEGS, LANES)),
                )
                states.append(est[rows(n), lane] + jnp.exp(r * (place.astype(F32) * (-float(STEPS)))) * enter)
            skip = jnp.broadcast_to(skip2[:, lane], (SEGS, LANES))
            out_lane = lanes(half)

            def step(i, states):
                pair = []
                for k in range(2):
                    u = uext[rows(2 * i + k), lane]
                    states = [decay[n] * states[n] + u for n in range(POLES)]
                    terms = [weight[n] * states[n] for n in range(POLES)]
                    while len(terms) > 1:
                        terms = [terms[a] + terms[a + 1] for a in range(0, len(terms), 2)]
                    pair.append(q32[rows(2 * i + k), lane] * (terms[0] + skip * u))
                zo[1, kh, pl.ds(pl.multiple_of(i * 16, 16), 16), out_lane] = jnp.concatenate(pair, axis=0).astype(BF16)
                return tuple(states)

            lax.fori_loop(0, STEPS // 2, step, tuple(states))

        z_copy(1, kh).start()

    project(1)

    @pl.loop(0, 32)
    def _(i):
        base = mid[t, i // 8, pl.ds(pl.multiple_of((i % 8) * 16, 16), 16), :].astype(F32)
        value = base + arrivals(1, i)
        for k in range(WIDTH // LANES):
            part = value[:, LANES * k : LANES * (k + 1)]
            x32[1, k, pl.ds(2 * i, SEGS, stride=STEPS), :] = part[:SEGS]
            x32[1, k, pl.ds(2 * i + 1, SEGS, stride=STEPS), :] = part[SEGS:]

    @pl.loop(0, 32)
    def _(i):
        s = i // 16
        r = (i % 16) * 16
        here = pl.ds(pl.multiple_of(i * 16, 16), 16)
        value = jnp.concatenate([x32[1, k, here, :] for k in range(WIDTH // LANES)], axis=1)
        obf[s, pl.ds(pl.multiple_of(r, 16), 16), :] = value.astype(BF16)

    store = pltpu.make_async_copy(obf, out_h, loc.at[3])
    store.start()

    tail_copy.wait_send()
    u_copy.wait_send()
    l_copy.wait_send()
    weight_drain(0, wo1_h)
    weight_drain(1, wo2_h)
    project_drain(0)
    project_drain(1)
    for copy in sent:
        copy.wait_send()
    for d in range(1, 16):

        @pl.when(c + d < 16)
        def _(d=d):
            state_copy(d).wait_send()

    store.wait()


def local(
    residual_in, mr_qkv, mr_short_w, mr_filter, mr_skip, mr_out_w, lr_gain,
    lr_in_w, lr_short_w, lr_rate, lr_res, lr_skip, lr_out_w,
):
    vmem = pl.BlockSpec(memory_space=pltpu.VMEM)
    hbm = pl.BlockSpec(memory_space=pl.ANY)
    dma = pltpu.SemaphoreType.DMA
    scratch = [
        pltpu.VMEM((2, 3, 256, WIDTH), BF16),
        pltpu.VMEM((2, 3, 8, WIDTH), BF16),
        pltpu.VMEM((3, WIDTH // LANES, ROWS, LANES), F32),
        pltpu.VMEM((ROWS, WIDTH), F32),
        pltpu.VMEM((192 * SEGS, WIDTH), F32),
        pltpu.VMEM((TAPS * SEGS, WIDTH), F32),
        pltpu.VMEM((256, WIDTH), BF16),
        pltpu.VMEM((256, WIDTH), BF16),
        pltpu.VMEM((2, 2, ROWS, 256), BF16),
        pltpu.VMEM((2, 2, ROWS, 256), BF16),
        pltpu.VMEM((2, 8, 2, WIDTH, 256), BF16),
        pltpu.VMEM((3, 4096, WIDTH), BF16),
        pltpu.VMEM((2, 3, ROWS, WIDTH), BF16),
        pltpu.VMEM((2, 3, ROWS, WIDTH), BF16),
        pltpu.VMEM((ROWS, WIDTH), F32),
        pltpu.VMEM((8, 4, 128, WIDTH), BF16),
        pltpu.VMEM((ROWS, WIDTH), BF16),
        pltpu.VMEM((3, ROWS, WIDTH), F32),
        pltpu.VMEM((ROWS, LANES), F32),
        pltpu.VMEM((3, 16, WIDTH), BF16),
        pltpu.VMEM((3, 16, WIDTH), BF16),
        pltpu.VMEM((POLES * SEGS, WIDTH), F32),
        pltpu.VMEM((4 * SEGS, WIDTH), BF16),
        pltpu.VMEM((15, 4 * SEGS, WIDTH), BF16),
        pltpu.VMEM((4 * SEGS, WIDTH), F32),
        pltpu.VMEM((2, 256, WIDTH), BF16),
        pltpu.VMEM((2, 256, WIDTH), BF16),
        dma((4,)),
        dma((3,)),
        dma((3,)),
        dma((2, 8)),
        dma((2, 8)),
        dma((2, 8, 2)),
        dma((2, 2)),
        dma((2, 2)),
        dma((2, 3)),
        dma((2, 3)),
        dma((32,)),
        dma((8, 4)),
        dma((15,)),
        dma((15,)),
    ]
    return pl.pallas_call(
        kernel,
        out_shape=jax.ShapeDtypeStruct((2, 256, WIDTH), BF16),
        in_specs=[hbm, hbm, vmem, vmem, vmem, hbm, vmem, hbm, vmem, vmem, vmem, vmem, hbm],
        out_specs=hbm,
        scratch_shapes=scratch,
        compiler_params=pltpu.CompilerParams(
            collective_id=0, has_side_effects=True, vmem_limit_bytes=62 * 1024 * 1024
        ),
    )(
        residual_in,
        jnp.transpose(mr_qkv, (0, 2, 1, 3)),
        mr_short_w.reshape(9, WIDTH),
        mr_filter,
        mr_skip.reshape(1, WIDTH),
        mr_out_w,
        lr_gain.reshape(8, WIDTH),
        jnp.transpose(lr_in_w, (1, 0, 2)),
        lr_short_w.reshape(9, WIDTH),
        lr_rate,
        lr_res,
        lr_skip.reshape(1, WIDTH),
        lr_out_w,
    )


def solution(mesh):
    in_specs = (
        P(None, "ctx", "tp"),
        P(None, "ctx", None, "tp"),
        P(None, None, "tp"),
        P(None, "tp"),
        P("tp"),
        P("tp", "ctx"),
        P(),
        P(None, None, "tp"),
        P(None, None, "tp"),
        P(None, "tp"),
        P(None, "tp"),
        P("tp"),
        P("tp", "ctx"),
    )
    return jax.shard_map(local, mesh=mesh, in_specs=in_specs, out_specs=P(None, "ctx", "tp"), check_vma=False)
```

profile of v0, /device:TPU:6, one launch (start us, length us, event | category | flops | bytes accessed | tf_op | source)
XLA Modules:
  0.0 223.3 jit_solution(9861354528556209119)
XLA Ops:
  0.0 1.3 reshape.17.gain
  1.3 1.4 reshape.15.sw1
  2.7 1.4 reshape.18.sw2
  4.0 217.4 %shard_map.127 = bf16[2,256,512]{2,1,0:T(8,128)(2,1)} custom-call(bf16[2,256,512]{2,1,0:T(8,128)(2,1)} %res_h.1, bf16[2,3,256,512]{3,2,1,0:T(8,128)(2,1)} %bitcast.5, f32[9,512]{1,0:T(8,128)} %reshape.15.sw1, bf16[128,512]{1,0:T(8,128)(2,1)} %filt.1, f32[1,512]{1,0:T(1,128)} %bitcast.6, bf16[512,256]{1,0:T(8,128)(2,1)} %wo1_h.1, f32[8,512]{1,0:T(8,128)} %reshape.17.gain, ...), custom_call_target="tpu_custom_call" | custom-call | tf_op jit(solution)/shard_map/pallas_call | solution.py:658
  221.4 1.9 copy.15
where the time goes:
time: 227 us; the launch traced here: 223 us
  Pallas kernels  217 us (96%)
  local copies, waits for them, and re-layouts  5.91 us (3%)
    pallas_call x1, Pallas kernels, local(): pl.pallas_call(kernel, out_shape=jax.ShapeDtypeStruct((2, 256, WIDTH), BF...  217 us

commit v1 on v0

--- a/solution.py
+++ b/solution.py
@@ -23,13 +23,14 @@
     out_h,
     qkv_v, xtail, x32, q32, uext, fb, pk_s, pk_r, zo, zn, w, win, ps, pr, pacc, mid, scaled, acc, ssq,
     ltail_s, ltail, est, st_s, st_r, hin, obf, resv,
-    loc, hs, hr, wsnd, fsnd, wrecv, zs, zr, pss, prs, ags, agr, sts, strv,
+    loc, hs, hr, wsnd, fsnd, bsnd, wrecv, zs, zr, pss, prs, ags, agr, sts, strv,
 ):
     c = lax.axis_index("ctx")
     t = lax.axis_index("tp")
     core = c % 2
     m = c // 2
     y = m % 4
+    xh = m // 4
     z = t // 2
     xl = t % 2
     sib = c + 1 - 2 * core
@@ -64,78 +65,128 @@
     for d in range(1, 16):
         greet((c + d) % 16, t)
     greet(c, xn)
-    for d in range(1, 4):
-        greet(c, ztp(d, xl))
-    for q in range(4):
-        greet(2 * (2 * q + xl) + core, xn)
-    pl.semaphore_wait(barrier, 19 + 8 * ((y + xl) % 2))
+    greet((c + 8) % 16, xn)
+    greet(c, ztp(1, xl))
+    greet(c, ztp(3, xl))
+    pl.semaphore_wait(barrier, 19)
 
     tail_copy = remote(qkv_h.at[:, :, 248:256, :], xtail, hs.at[0], hr.at[0], (c + 1) % 16, t)
     tail_copy.start()
 
-    slot_mine = xl * 4 + m // 2
-    same = (y + xl) % 2 == 0
-
-    def weight_copies(stage, source):
-        home = pltpu.make_async_copy(source, w.at[stage, slot_mine, core], wrecv.at[stage, slot_mine, core])
-        far = [
-            remote(
-                source,
-                w.at[stage, slot_mine, core],
-                wsnd.at[stage, d],
-                wrecv.at[stage, slot_mine, core],
-                2 * ((m + d) % 8) + core,
-                2 * z + y % 2,
-            )
-            for d in range(8)
+    holder = (y + xl) % 2 == 0
+    relay = (y + xl) % 2 == 1
+    ups = ((y + 1) % 4, (y + 3) % 4)
+
+    def place_of(k, row):
+        xs = (xl, 1 - xl, 1 - xl, xl)[k]
+        xhs = (xh, xh, 1 - xh, 1 - xh)[k]
+        return xs * 4 + xhs * 2 + row // 2
+
+    def ctx_of(h, row):
+        return (h * 4 + row) * 2 + core
+
+    def weight_first(stage, source):
+        mine = place_of(0, y)
+        target = w.at[stage, mine, core]
+        arrival = wrecv.at[stage, mine, core]
+        home = pltpu.make_async_copy(source, target, arrival)
+        along = [
+            remote(source, target, wsnd.at[stage, 0], arrival, ctx_of(xh, ups[0]), t),
+            remote(source, target, wsnd.at[stage, 1], arrival, ctx_of(xh, ups[1]), t),
+            remote(source, target, wsnd.at[stage, 2], arrival, ctx_of(1 - xh, y), t),
         ]
-        return home, far
+        across = [
+            remote(source, target, wsnd.at[stage, 0], arrival, c, xn),
+            remote(source, target, wsnd.at[stage, 1], arrival, ctx_of(1 - xh, y), xn),
+        ]
+        return home, along, across
 
     def weight_start(stage, source):
-        home, far = weight_copies(stage, source)
-        for d in (4, 2, 6, 1, 3, 5, 7):
-            far[d].start()
-
-        @pl.when(same)
+        home, along, across = weight_first(stage, source)
+
+        @pl.when(holder)
         def _():
             home.start()
-
-        @pl.when(jnp.logical_not(same))
+            for copy in along:
+                copy.start()
+
+        @pl.when(relay)
         def _():
-            far[0].start()
-
-    def weight_forward(stage, index):
+            for copy in across:
+                copy.start()
+
+    def weight_pass(stage, index, sem, ctx):
+        block = w.at[stage, index, core]
+        return remote(block, block, sem, wrecv.at[stage, index, core], ctx, t)
+
+    def weight_got(stage, index):
         arrived(w.at[stage, index, core], wrecv.at[stage, index, core])
-        remote(
-            w.at[stage, index, core],
-            w.at[stage, index, core],
-            fsnd.at[stage, index],
-            wrecv.at[stage, index, core],
-            sib,
-            t,
-        ).start()
+
+    def weight_moves(stage, k):
+        here, up, down, far = place_of(k, y), place_of(k, ups[0]), place_of(k, ups[1]), place_of(k, (y + 2) % 4)
+
+        def sibling(index, n):
+            return weight_pass(stage, index, bsnd.at[stage, n], sib)
+
+        held = [sibling(here, k)]
+        if k:
+            held += [weight_pass(stage, here, fsnd.at[stage, n, k], ctx_of(xh, ups[n])) for n in range(2)]
+        late = [sibling(far, 4 + k)]
+        below = [sibling(down, k)]
+        above = [sibling(up, 4 + k)]
+        if k % 2 == 0:
+            below.append(weight_pass(stage, down, fsnd.at[stage, 0, k], ctx_of(xh, ups[0])))
+        else:
+            above.append(weight_pass(stage, up, fsnd.at[stage, 0, k], ctx_of(xh, ups[1])))
+        return (here, held), (far, late), (down, below), (up, above)
+
+    def weight_step(stage, k):
+        first_, _, below, above = weight_moves(stage, k)
+
+        @pl.when(holder)
+        def _():
+            weight_got(stage, first_[0])
+            for copy in reversed(first_[1]):
+                copy.start()
+
+        @pl.when(relay)
+        def _():
+            for index, copies in (below, above):
+                weight_got(stage, index)
+                for copy in reversed(copies):
+                    copy.start()
+
+    def weight_last(stage):
+        @pl.when(holder)
+        def _():
+            for k in range(4):
+                _, (index, copies), _, _ = weight_moves(stage, k)
+                weight_got(stage, index)
+                copies[0].start()
 
     def weight_sibling(stage, index):
         arrived(w.at[stage, index, 1 - core], wrecv.at[stage, index, 1 - core])
 
     def weight_drain(stage, source):
-        _, far = weight_copies(stage, source)
-        for d in range(1, 8):
-            far[d].wait_send()
-
-        @pl.when(jnp.logical_not(same))
+        _, along, across = weight_first(stage, source)
+
+        @pl.when(holder)
         def _():
-            far[0].wait_send()
-
-        for index in range(8):
-            remote(
-                w.at[stage, index, core],
-                w.at[stage, index, core],
-                fsnd.at[stage, index],
-                wrecv.at[stage, index, core],
-                sib,
-                t,
-            ).wait_send()
+            for copy in along:
+                copy.wait_send()
+            for k in range(4):
+                first_, late, _, _ = weight_moves(stage, k)
+                for copy in first_[1] + late[1]:
+                    copy.wait_send()
+
+        @pl.when(relay)
+        def _():
+            for copy in across:
+                copy.wait_send()
+            for k in range(4):
+                _, _, below, above = weight_moves(stage, k)
+                for copy in below[1] + above[1]:
+                    copy.wait_send()
 
     weight_start(0, wo1_h)
     load_win = pltpu.make_async_copy(win_h, win, loc.at[2])
@@ -171,7 +222,7 @@
                     x32[p, k, there, :] = values[:, LANES * k : LANES * (k + 1)]
 
     def tap(ref, lag, p):
-        return jnp.broadcast_to(ref[3 * lag + p : 3 * lag + p + 1, :], (SEGS, WIDTH))
+        return jnp.broadcast_to(ref[lag, p : p + 1, :], (SEGS, WIDTH))
 
     def strided3(p, j):
         return jnp.concatenate(
@@ -212,6 +263,7 @@
 
     u_copy = remote(pk_s, pk_r, hs.at[1], hr.at[1], (c + 1) % 16, t)
     u_copy.start()
+    weight_step(0, 0)
 
     arrived(xtail, hr.at[0])
 
@@ -239,54 +291,60 @@
         uext[rows(2 * i), :] = jnp.where(seg % 4 < 2, pltpu.roll(got, 6, 0), pltpu.roll(even, 2, 0))
         uext[rows(1 + 2 * i), :] = jnp.where(seg % 4 < 2, got, pltpu.roll(odd, 2, 0))
 
+    weight_step(0, 1)
+
     def z_copy(stage, kh):
         return remote(zo.at[stage, kh], zn.at[stage, kh], zs.at[stage, kh], zr.at[stage, kh], c, xn)
 
-    def p_copy(stage, d):
+    def p_copy(stage, i):
         return remote(
-            ps.at[stage, d - 1], pr.at[stage, d - 1], pss.at[stage, d - 1], prs.at[stage, d - 1], c, ztp(d, xl)
+            ps.at[stage, i], pr.at[stage, i], pss.at[stage, i], prs.at[stage, i], c, ztp(1 if i % 2 == 0 else 3, xl)
         )
 
     def project(stage):
         for kh in range(2):
             arrived(zn.at[stage, kh], zr.at[stage, kh])
-        for d in (2, 1, 3, 0):
+
+        def term(d, half):
             dest = (z + d) % 4
-            for source in range(2):
-                weight_sibling(stage, source * 4 + dest)
-
-            @pl.loop(0, 2)
-            def _(half, d=d, dest=dest):
-                mine = xl * 4 + dest
-                other = (1 - xl) * 4 + dest
-                total = jnp.zeros((ROWS, 256), F32)
-                for kh in range(2):
-                    ks = pl.ds(256 * kh, 256)
-                    total += jnp.dot(zo[stage, kh], w[stage, mine, half, ks, :], preferred_element_type=F32)
-                    total += jnp.dot(zn[stage, kh], w[stage, other, half, ks, :], preferred_element_type=F32)
-                cols = pl.ds(pl.multiple_of(half * 256, 256), 256)
-                if d == 0:
-                    pacc[:, cols] = total
-                else:
-                    ps[stage, d - 1, :, cols] = total.astype(BF16)
-
-            if d:
-                p_copy(stage, d).start()
-        for d in (1, 3, 2):
-            arrived(pr.at[stage, d - 1], prs.at[stage, d - 1])
+            total = jnp.zeros((ROWS, 256), F32)
+            for kh in range(2):
+                ks = pl.ds(256 * kh, 256)
+                total += jnp.dot(zo[stage, kh], w[stage, xl * 4 + dest, half, ks, :], preferred_element_type=F32)
+                total += jnp.dot(zn[stage, kh], w[stage, (1 - xl) * 4 + dest, half, ks, :], preferred_element_type=F32)
+            return total
+
+        for i, d, half in ((0, 2, 0), (1, 2, 1), (2, 1, 1), (3, 3, 0), (4, 1, 0), (5, 3, 1)):
+            if i in (0, 2, 3):
+                for source in range(2):
+                    weight_sibling(stage, source * 4 + (z + d) % 4)
+            if i >= 4:
+                arrived(pr.at[stage, i - 4], prs.at[stage, i - 4])
+                ps[stage, i] = (term(d, half) + pr[stage, i - 4].astype(F32)).astype(BF16)
+            else:
+                ps[stage, i] = term(d, half).astype(BF16)
+            p_copy(stage, i).start()
+            if i == 3:
+                for source in range(2):
+                    weight_sibling(stage, source * 4 + z)
+                for own in range(2):
+                    pacc[:, 256 * own : 256 * (own + 1)] = term(0, own)
+
+    def project_wait(stage):
+        for i in (2, 3, 4, 5):
+            arrived(pr.at[stage, i], prs.at[stage, i])
 
     def project_drain(stage):
         for kh in range(2):
             z_copy(stage, kh).wait_send()
-        for d in range(1, 4):
-            p_copy(stage, d).wait_send()
+        for i in range(6):
+            p_copy(stage, i).wait_send()
 
     def arrivals(stage, i):
         here = pl.ds(pl.multiple_of(i * 16, 16), 16)
-        total = pacc[here, :]
-        for k in range(3):
-            total += pr[stage, k, here, :].astype(F32)
-        return total
+        left = pr[stage, 3, here, :].astype(F32) + pr[stage, 4, here, :].astype(F32)
+        right = pr[stage, 2, here, :].astype(F32) + pr[stage, 5, here, :].astype(F32)
+        return pacc[here, :] + jnp.concatenate([left, right], axis=1)
 
     for kh in range(2):
 
@@ -320,12 +378,14 @@
                 ).astype(BF16)
 
         z_copy(0, kh).start()
-
-    for d in (2, 1, 3, 0):
-        for source in range(2):
-            weight_forward(0, source * 4 + (z + d) % 4)
+        weight_step(0, 2 + kh)
+
+    weight_start(1, wo2_h)
+    weight_last(0)
     project(0)
-    weight_start(1, wo2_h)
+    weight_step(1, 0)
+    weight_step(1, 1)
+    project_wait(0)
 
     load_res.wait()
 
@@ -360,7 +420,7 @@
     load_win.wait()
 
     def absorb(slot, fresh=False):
-        scale = gain[pl.ds(slot, 1), :]
+        scale = gain[:, pl.ds(pl.multiple_of(slot * WIDTH, WIDTH), WIDTH)]
 
         @pl.loop(0, 16)
         def _(i):
@@ -386,6 +446,7 @@
         send(t, quarter, zp)
         send(t, quarter, zm)
     absorb(t, fresh=True)
+    weight_step(1, 2)
     have(xn, 0, 1)
     for quarter in range(2):
         send(xn, quarter, zp)
@@ -401,6 +462,7 @@
     send(zp, 2, xn)
     send(zp, 3, xn)
     absorb(zm)
+    weight_step(1, 3)
     absorb(zp)
     have(xm, 0, 1)
     send(xm, 0, zp)
@@ -419,9 +481,7 @@
     have(xz, 0, 1, 2, 3)
     absorb(xz)
 
-    for d in (2, 1, 3, 0):
-        for source in range(2):
-            weight_forward(1, source * 4 + (z + d) % 4)
+    weight_last(1)
 
     def finish(i):
         here = pl.ds(i * 16 if isinstance(i, int) else pl.multiple_of(i * 16, 16), 16)
@@ -566,6 +626,7 @@
         z_copy(1, kh).start()
 
     project(1)
+    project_wait(1)
 
     @pl.loop(0, 32)
     def _(i):
@@ -625,8 +686,8 @@
         pltpu.VMEM((2, 2, ROWS, 256), BF16),
         pltpu.VMEM((2, 8, 2, WIDTH, 256), BF16),
         pltpu.VMEM((3, 4096, WIDTH), BF16),
-        pltpu.VMEM((2, 3, ROWS, WIDTH), BF16),
-        pltpu.VMEM((2, 3, ROWS, WIDTH), BF16),
+        pltpu.VMEM((2, 6, ROWS, 256), BF16),
+        pltpu.VMEM((2, 6, ROWS, 256), BF16),
         pltpu.VMEM((ROWS, WIDTH), F32),
         pltpu.VMEM((8, 4, 128, WIDTH), BF16),
         pltpu.VMEM((ROWS, WIDTH), BF16),
@@ -643,13 +704,14 @@
         dma((4,)),
         dma((3,)),
         dma((3,)),
-        dma((2, 8)),
+        dma((2, 3)),
+        dma((2, 2, 4)),
         dma((2, 8)),
         dma((2, 8, 2)),
         dma((2, 2)),
         dma((2, 2)),
-        dma((2, 3)),
-        dma((2, 3)),
+        dma((2, 6)),
+        dma((2, 6)),
         dma((32,)),
         dma((8, 4)),
         dma((15,)),
@@ -667,13 +729,13 @@
     )(
         residual_in,
         jnp.transpose(mr_qkv, (0, 2, 1, 3)),
-        mr_short_w.reshape(9, WIDTH),
+        mr_short_w,
         mr_filter,
         mr_skip.reshape(1, WIDTH),
         mr_out_w,
-        lr_gain.reshape(8, WIDTH),
+        lr_gain.reshape(1, 8 * WIDTH),
         jnp.transpose(lr_in_w, (1, 0, 2)),
-        lr_short_w.reshape(9, WIDTH),
+        lr_short_w,
         lr_rate,
         lr_res,
         lr_skip.reshape(1, WIDTH),

time: 227 us -> 162 us (0.71)
  Pallas kernels: 217 us -> 158 us
  local copies, waits for them, and re-layouts: 5.91 us -> 1.87 us
    pallas_call x1, Pallas kernels: 217 us -> 158 us  [local(): pl.pallas_call(kernel, out_shape=jax.ShapeDtypeStruct((2, 256, WIDTH), BF...]
    reshape x3 -> x0, local copies, waits for them, and re-layouts: 4.04 us -> none  [the longest x1 1.36 us: local(): mr_short_w.reshape(9, WIDTH)]
where the time goes in v1:
time: 162 us; the launch traced here: 160 us
  Pallas kernels  158 us (98%)
  local copies, waits for them, and re-layouts  1.87 us (1%)
    pallas_call x1, Pallas kernels, local(): pl.pallas_call(kernel, out_shape=jax.ShapeDtypeStruct((2, 256, WIDTH), BF...  158 us

profile of v1, /device:TPU:6, one launch (start us, length us, event | category | flops | bytes accessed | tf_op | source)
XLA Modules:
  0.0 159.9 jit_solution(8819586425983100904)
XLA Ops:
  0.0 158.0 %shard_map.127 = bf16[2,256,512]{2,1,0:T(8,128)(2,1)} custom-call(bf16[2,256,512]{2,1,0:T(8,128)(2,1)} %res_h.1, bf16[2,3,256,512]{3,2,1,0:T(8,128)(2,1)} %bitcast.6, f32[3,3,512]{2,1,0:T(4,128)} %sw1.1, bf16[128,512]{1,0:T(8,128)(2,1)} %filt.1, f32[1,512]{1,0:T(1,128)} %bitcast.8, bf16[512,256]{1,0:T(8,128)(2,1)} %wo1_h.1, f32[1,4096]{1,0:T(1,128)} %bitcast.7, ...), custom_call_target="tpu_custom_call" | custom-call | tf_op jit(solution)/shard_map/pallas_call | solution.py:720
  158.0 1.9 %copy.15 = bf16[2,256,512]{2,1,0:T(8,128)(2,1)} copy(bf16[2,256,512]{2,1,0:T(8,128)(2,1)} %shard_map.127) | data formatting | bytes 1048576

commit v2 on v1

--- a/solution.py
+++ b/solution.py
@@ -140,14 +140,17 @@
             above.append(weight_pass(stage, up, fsnd.at[stage, 0, k], ctx_of(xh, ups[1])))
         return (here, held), (far, late), (down, below), (up, above)
 
-    def weight_step(stage, k):
-        first_, _, below, above = weight_moves(stage, k)
-
+    def weight_hold(stage, *ks):
         @pl.when(holder)
         def _():
-            weight_got(stage, first_[0])
-            for copy in reversed(first_[1]):
-                copy.start()
+            for k in ks:
+                first_ = weight_moves(stage, k)[0]
+                weight_got(stage, first_[0])
+                for copy in reversed(first_[1]):
+                    copy.start()
+
+    def weight_relay(stage, k):
+        _, _, below, above = weight_moves(stage, k)
 
         @pl.when(relay)
         def _():
@@ -243,14 +246,13 @@
     medium(0, x0, own1, own2)
     medium(1, x1, x0, own1)
 
-    @pl.loop(2, STEPS)
-    def _(j):
-        medium(
-            j,
-            [strided3(p, j) for p in range(3)],
-            [strided3(p, j - 1) for p in range(3)],
-            [strided3(p, j - 2) for p in range(3)],
-        )
+    def medium_step(j, carried):
+        now = [strided3(p, j) for p in range(3)]
+        before, before2 = carried
+        medium(j, now, before, before2)
+        return now, before
+
+    lax.fori_loop(2, STEPS, medium_step, (x1, x0))
 
     @pl.loop(0, STEPS // 4)
     def _(i):
@@ -263,7 +265,8 @@
 
     u_copy = remote(pk_s, pk_r, hs.at[1], hr.at[1], (c + 1) % 16, t)
     u_copy.start()
-    weight_step(0, 0)
+    weight_hold(0, 0)
+    weight_relay(0, 0)
 
     arrived(xtail, hr.at[0])
 
@@ -291,67 +294,84 @@
         uext[rows(2 * i), :] = jnp.where(seg % 4 < 2, pltpu.roll(got, 6, 0), pltpu.roll(even, 2, 0))
         uext[rows(1 + 2 * i), :] = jnp.where(seg % 4 < 2, got, pltpu.roll(odd, 2, 0))
 
-    weight_step(0, 1)
-
-    def z_copy(stage, kh):
-        return remote(zo.at[stage, kh], zn.at[stage, kh], zs.at[stage, kh], zr.at[stage, kh], c, xn)
-
-    def p_copy(stage, i):
+    weight_hold(0, 1, 2)
+
+    HALF = ROWS // 2
+
+    def z_copy(stage, part):
+        return remote(zo.at[stage, part], zn.at[stage, part], zs.at[stage, part], zr.at[stage, part], c, xn)
+
+    def p_copy(stage, part, i):
         return remote(
-            ps.at[stage, i], pr.at[stage, i], pss.at[stage, i], prs.at[stage, i], c, ztp(1 if i % 2 == 0 else 3, xl)
+            ps.at[stage, part, i],
+            pr.at[stage, part, i],
+            pss.at[stage, part, i],
+            prs.at[stage, part, i],
+            c,
+            ztp(1 if i % 2 == 0 else 3, xl),
         )
 
-    def project(stage):
-        for kh in range(2):
-            arrived(zn.at[stage, kh], zr.at[stage, kh])
-
-        def term(d, half):
-            dest = (z + d) % 4
-            total = jnp.zeros((ROWS, 256), F32)
-            for kh in range(2):
-                ks = pl.ds(256 * kh, 256)
-                total += jnp.dot(zo[stage, kh], w[stage, xl * 4 + dest, half, ks, :], preferred_element_type=F32)
-                total += jnp.dot(zn[stage, kh], w[stage, (1 - xl) * 4 + dest, half, ks, :], preferred_element_type=F32)
-            return total
-
-        for i, d, half in ((0, 2, 0), (1, 2, 1), (2, 1, 1), (3, 3, 0), (4, 1, 0), (5, 3, 1)):
-            if i in (0, 2, 3):
+    def term(stage, part, d, half):
+        dest = (z + d) % 4
+        both = jnp.concatenate([zo[stage, part], zn[stage, part]], axis=1)
+        weights = jnp.concatenate([w[stage, xl * 4 + dest, half], w[stage, (1 - xl) * 4 + dest, half]], axis=0)
+        return jnp.dot(both, weights, preferred_element_type=F32)
+
+    def project_first(stage, part):
+        arrived(zn.at[stage, part], zr.at[stage, part])
+        for i, d, half in ((0, 2, 0), (1, 2, 1), (2, 1, 1), (3, 3, 0)):
+            if part == 0 and i in (0, 2, 3):
                 for source in range(2):
                     weight_sibling(stage, source * 4 + (z + d) % 4)
-            if i >= 4:
-                arrived(pr.at[stage, i - 4], prs.at[stage, i - 4])
-                ps[stage, i] = (term(d, half) + pr[stage, i - 4].astype(F32)).astype(BF16)
-            else:
-                ps[stage, i] = term(d, half).astype(BF16)
-            p_copy(stage, i).start()
-            if i == 3:
-                for source in range(2):
-                    weight_sibling(stage, source * 4 + z)
-                for own in range(2):
-                    pacc[:, 256 * own : 256 * (own + 1)] = term(0, own)
-
-    def project_wait(stage):
+            ps[stage, part, i] = term(stage, part, d, half).astype(BF16)
+            p_copy(stage, part, i).start()
+
+    def project_own(stage, part):
+        if part == 0:
+            for source in range(2):
+                weight_sibling(stage, source * 4 + z)
+        for own in range(2):
+            pacc[HALF * part : HALF * (part + 1), 256 * own : 256 * (own + 1)] = term(stage, part, 0, own)
+
+    def project_relay(stage, part):
+        for i, d, half in ((4, 1, 0), (5, 3, 1)):
+            mine = term(stage, part, d, half)
+            arrived(pr.at[stage, part, i - 4], prs.at[stage, part, i - 4])
+            ps[stage, part, i] = (mine + pr[stage, part, i - 4].astype(F32)).astype(BF16)
+            p_copy(stage, part, i).start()
+
+    def project(stage):
+        project_first(stage, 0)
+        project_first(stage, 1)
+        project_relay(stage, 0)
+        project_own(stage, 0)
+        project_relay(stage, 1)
+        project_own(stage, 1)
+
+    def project_wait(stage, part):
         for i in (2, 3, 4, 5):
-            arrived(pr.at[stage, i], prs.at[stage, i])
+            arrived(pr.at[stage, part, i], prs.at[stage, part, i])
 
     def project_drain(stage):
-        for kh in range(2):
-            z_copy(stage, kh).wait_send()
-        for i in range(6):
-            p_copy(stage, i).wait_send()
-
-    def arrivals(stage, i):
+        for part in range(2):
+            z_copy(stage, part).wait_send()
+            for i in range(6):
+                p_copy(stage, part, i).wait_send()
+
+    def arrivals(stage, part, i):
         here = pl.ds(pl.multiple_of(i * 16, 16), 16)
-        left = pr[stage, 3, here, :].astype(F32) + pr[stage, 4, here, :].astype(F32)
-        right = pr[stage, 2, here, :].astype(F32) + pr[stage, 5, here, :].astype(F32)
-        return pacc[here, :] + jnp.concatenate([left, right], axis=1)
-
-    for kh in range(2):
-
-        @pl.loop(0, 8)
-        def _(block, kh=kh):
-            lane = lanes(kh * 2 + block // 4)
-            j0 = (block % 4) * 16
+        left = pr[stage, part, 3, here, :].astype(F32) + pr[stage, part, 4, here, :].astype(F32)
+        right = pr[stage, part, 2, here, :].astype(F32) + pr[stage, part, 5, here, :].astype(F32)
+        own = pacc[pl.ds(pl.multiple_of(part * HALF + i * 16, 16), 16), :]
+        return own + jnp.concatenate([left, right], axis=1)
+
+    def filter_blocks(first_block):
+        @pl.loop(first_block, first_block + 4)
+        def _(block):
+            lane = lanes((block % 8) // 2)
+            part = block // 8
+            r0 = (block % 2) * 16
+            j0 = part * 32 + r0
 
             def taps8(ib, totals):
                 base = 128 + j0 - 8 * ib - 7
@@ -367,25 +387,27 @@
 
             totals = lax.fori_loop(0, 16, taps8, tuple(jnp.zeros((SEGS, LANES), F32) for _ in range(16)))
             skip = jnp.broadcast_to(skip1[:, lane], (SEGS, LANES))
-            out_lane = lanes(block // 4)
             for a in range(0, 16, 2):
                 pair = []
                 for k in (a, a + 1):
                     u = uext[rows(128 + j0 + k), lane]
                     pair.append(q32[rows(j0 + k), lane] * (totals[k] + skip * u))
-                zo[0, kh, pl.ds(pl.multiple_of((j0 + a) * SEGS, 16), 16), out_lane] = jnp.concatenate(
+                zo[0, part, pl.ds(pl.multiple_of((r0 + a) * SEGS, 16), 16), lane] = jnp.concatenate(
                     pair, axis=0
                 ).astype(BF16)
 
-        z_copy(0, kh).start()
-        weight_step(0, 2 + kh)
-
+    filter_blocks(0)
+    weight_hold(0, 3)
+    weight_relay(0, 1)
+    filter_blocks(4)
+    z_copy(0, 0).start()
+    weight_relay(0, 2)
+    filter_blocks(8)
+    filter_blocks(12)
+    z_copy(0, 1).start()
+    weight_relay(0, 3)
+    weight_last(0)
     weight_start(1, wo2_h)
-    weight_last(0)
-    project(0)
-    weight_step(1, 0)
-    weight_step(1, 1)
-    project_wait(0)
 
     load_res.wait()
 
@@ -397,11 +419,14 @@
         for k in range(WIDTH // LANES):
             x32[0, k, pl.ds(pl.multiple_of(i * 16, 16), 16), :] = values[:, LANES * k : LANES * (k + 1)]
 
-    @pl.loop(0, 32)
-    def _(i):
-        before = jnp.concatenate([strided3(0, 2 * i), strided3(0, 2 * i + 1)], axis=0)
-        value = (before + arrivals(0, i)).astype(BF16)
-        mid[t, i // 8, pl.ds(pl.multiple_of((i % 8) * 16, 16), 16), :] = value
+    @pl.loop(0, STEPS)
+    def _(j):
+        for k in range(WIDTH // LANES):
+            x32[1, k, rows(j), :] = x32[0, k, pl.ds(j, SEGS, stride=STEPS), :]
+
+    project(0)
+    weight_hold(1, 0, 1, 2)
+    weight_relay(1, 0)
 
     sent = []
 
@@ -413,40 +438,57 @@
         copy.start()
         sent.append(copy)
 
+    zp, zm, zz = ztp(1, xl), ztp(3, xl), ztp(2, xl)
+    xp, xm, xz = ztp(1, 1 - xl), ztp(3, 1 - xl), ztp(2, 1 - xl)
+    for part in range(2):
+        project_wait(0, part)
+
+        @pl.loop(0, 16)
+        def _(i, part=part):
+            here = pl.ds(pl.multiple_of(part * HALF + i * 16, 16), 16)
+            before = jnp.concatenate([x32[1, k, here, :] for k in range(WIDTH // LANES)], axis=1)
+            value = (before + arrivals(0, part, i)).astype(BF16)
+            mid[t, part * 2 + i // 8, pl.ds(pl.multiple_of((i % 8) * 16, 16), 16), :] = value
+
+        for quarter in (2 * part, 2 * part + 1):
+            send(t, quarter, xn)
+            send(t, quarter, zp)
+            send(t, quarter, zm)
+
     def have(slot, *quarters):
         for quarter in quarters:
             arrived(mid.at[slot, quarter], agr.at[slot, quarter])
 
     load_win.wait()
 
-    def absorb(slot, fresh=False):
-        scale = gain[:, pl.ds(pl.multiple_of(slot * WIDTH, WIDTH), WIDTH)]
+    def absorb(*slots, fresh=False):
+        count = len(slots)
+        scales = [gain[:, pl.ds(pl.multiple_of(slot * WIDTH, WIDTH), WIDTH)] for slot in slots]
 
         @pl.loop(0, 16)
         def _(i):
             here = pl.ds(pl.multiple_of((i % 4) * 32, 32), 32)
-            values = mid[slot, i // 4, here, :].astype(F32)
-            square = values * values
-            part = square[:, 0:128] + square[:, 128:256] + square[:, 256:384] + square[:, 384:512]
             there = pl.ds(pl.multiple_of(i * 32, 32), 32)
-            ssq[there, :] = part if fresh else ssq[there, :] + part
-            scaled[there, :] = (values * scale).astype(BF16)
+            total = 0.0 if fresh else ssq[there, :]
+            for k, slot in enumerate(slots):
+                values = mid[slot, i // 4, here, :].astype(F32)
+                square = values * values
+                total += square[:, 0:128] + square[:, 128:256] + square[:, 256:384] + square[:, 384:512]
+                scaled[there, WIDTH * k : WIDTH * (k + 1)] = (values * scales[k]).astype(BF16)
+            ssq[there, :] = total
 
         @pl.loop(0, 6)
         def _(i):
             cols = pl.ds(pl.multiple_of((i % 2) * 256, 256), 256)
-            depth = pl.ds(pl.multiple_of(slot * WIDTH, WIDTH), WIDTH)
-            product = jnp.dot(scaled[...], win[i // 2, depth, cols], preferred_element_type=F32)
+            weights = [win[i // 2, pl.ds(pl.multiple_of(slot * WIDTH, WIDTH), WIDTH), cols] for slot in slots]
+            product = jnp.dot(
+                scaled[:, 0 : WIDTH * count], jnp.concatenate(weights, axis=0), preferred_element_type=F32
+            )
             acc[i // 2, :, cols] = product if fresh else acc[i // 2, :, cols] + product
 
-    zp, zm, zz = ztp(1, xl), ztp(3, xl), ztp(2, xl)
-    xp, xm, xz = ztp(1, 1 - xl), ztp(3, 1 - xl), ztp(2, 1 - xl)
-    for quarter in range(4):
-        send(t, quarter, xn)
-        send(t, quarter, zp)
-        send(t, quarter, zm)
     absorb(t, fresh=True)
-    weight_step(1, 2)
+    weight_hold(1, 3)
+    weight_relay(1, 1)
     have(xn, 0, 1)
     for quarter in range(2):
         send(xn, quarter, zp)
@@ -461,9 +503,8 @@
     send(zp, 3, zm)
     send(zp, 2, xn)
     send(zp, 3, xn)
-    absorb(zm)
-    weight_step(1, 3)
-    absorb(zp)
+    absorb(zm, zp)
+    weight_relay(1, 2)
     have(xm, 0, 1)
     send(xm, 0, zp)
     have(xp, 0, 1)
@@ -472,15 +513,13 @@
     send(zz, 2, xn)
     send(zz, 3, xn)
     have(xn, 2, 3)
-    absorb(xn)
-    absorb(zz)
+    absorb(xn, zz)
+    weight_relay(1, 3)
     have(xm, 2, 3)
-    absorb(xm)
     have(xp, 2, 3)
-    absorb(xp)
+    absorb(xm, xp)
     have(xz, 0, 1, 2, 3)
     absorb(xz)
-
     weight_last(1)
 
     def finish(i):
@@ -589,60 +628,68 @@
             arrived(st_r.at[d - 1], strv.at[d - 1])
             hin[...] += jnp.exp(pack * (-256.0 * (d - 1))) * st_r[d - 1].astype(F32)
 
-    for kh in range(2):
-
-        @pl.loop(0, 2)
-        def _(half, kh=kh):
-            lane = lanes(kh * 2 + half)
+    for part in range(2):
+
+        @pl.loop(0, WIDTH // LANES)
+        def _(lt, part=part):
+            lane = lanes(lt)
             decay, weight, states = [], [], []
             for n in range(POLES):
                 r = row_of(rate, n, lane)
                 decay.append(jnp.exp(-r))
                 weight.append(row_of(resid, n, lane) * jnp.sqrt(1.0 - jnp.exp(-2.0 * r)))
-                k = (n // 4) * SEGS + n % 4
-                enter = jnp.where(
-                    seg1 < 4,
-                    jnp.broadcast_to(hin[k : k + 1, lane], (SEGS, LANES)),
-                    jnp.broadcast_to(hin[k + 4 : k + 5, lane], (SEGS, LANES)),
-                )
-                states.append(est[rows(n), lane] + jnp.exp(r * (place.astype(F32) * (-float(STEPS)))) * enter)
+                state = est[rows(n), lane]
+                if part == 0:
+                    k = (n // 4) * SEGS + n % 4
+                    enter = jnp.where(
+                        seg1 < 4,
+                        jnp.broadcast_to(hin[k : k + 1, lane], (SEGS, LANES)),
+                        jnp.broadcast_to(hin[k + 4 : k + 5, lane], (SEGS, LANES)),
+                    )
+                    state = state + jnp.exp(r * (place.astype(F32) * (-float(STEPS)))) * enter
+                states.append(state)
             skip = jnp.broadcast_to(skip2[:, lane], (SEGS, LANES))
-            out_lane = lanes(half)
 
             def step(i, states):
                 pair = []
                 for k in range(2):
-                    u = uext[rows(2 * i + k), lane]
+                    j = part * (STEPS // 2) + 2 * i + k
+                    u = uext[rows(j), lane]
                     states = [decay[n] * states[n] + u for n in range(POLES)]
                     terms = [weight[n] * states[n] for n in range(POLES)]
                     while len(terms) > 1:
                         terms = [terms[a] + terms[a + 1] for a in range(0, len(terms), 2)]
-                    pair.append(q32[rows(2 * i + k), lane] * (terms[0] + skip * u))
-                zo[1, kh, pl.ds(pl.multiple_of(i * 16, 16), 16), out_lane] = jnp.concatenate(pair, axis=0).astype(BF16)
+                    pair.append(q32[rows(j), lane] * (terms[0] + skip * u))
+                zo[1, part, pl.ds(pl.multiple_of(i * 16, 16), 16), lane] = jnp.concatenate(pair, axis=0).astype(BF16)
                 return tuple(states)
 
-            lax.fori_loop(0, STEPS // 2, step, tuple(states))
-
-        z_copy(1, kh).start()
+            states = lax.fori_loop(0, STEPS // 4, step, tuple(states))
+            if part == 0:
+                for n in range(POLES):
+                    est[rows(n), lane] = states[n]
+
+        z_copy(1, part).start()
 
     project(1)
-    project_wait(1)
-
-    @pl.loop(0, 32)
-    def _(i):
-        base = mid[t, i // 8, pl.ds(pl.multiple_of((i % 8) * 16, 16), 16), :].astype(F32)
-        value = base + arrivals(1, i)
-        for k in range(WIDTH // LANES):
-            part = value[:, LANES * k : LANES * (k + 1)]
-            x32[1, k, pl.ds(2 * i, SEGS, stride=STEPS), :] = part[:SEGS]
-            x32[1, k, pl.ds(2 * i + 1, SEGS, stride=STEPS), :] = part[SEGS:]
+    for part in range(2):
+        project_wait(1, part)
+
+        @pl.loop(0, 16)
+        def _(i, part=part):
+            base = mid[t, part * 2 + i // 8, pl.ds(pl.multiple_of((i % 8) * 16, 16), 16), :].astype(F32)
+            value = base + arrivals(1, part, i)
+            j = part * (STEPS // 2) + 2 * i
+            for k in range(WIDTH // LANES):
+                piece = value[:, LANES * k : LANES * (k + 1)]
+                x32[2, k, pl.ds(j, SEGS, stride=STEPS), :] = piece[:SEGS]
+                x32[2, k, pl.ds(j + 1, SEGS, stride=STEPS), :] = piece[SEGS:]
 
     @pl.loop(0, 32)
     def _(i):
         s = i // 16
         r = (i % 16) * 16
         here = pl.ds(pl.multiple_of(i * 16, 16), 16)
-        value = jnp.concatenate([x32[1, k, here, :] for k in range(WIDTH // LANES)], axis=1)
+        value = jnp.concatenate([x32[2, k, here, :] for k in range(WIDTH // LANES)], axis=1)
         obf[s, pl.ds(pl.multiple_of(r, 16), 16), :] = value.astype(BF16)
 
     store = pltpu.make_async_copy(obf, out_h, loc.at[3])
@@ -682,15 +729,15 @@
         pltpu.VMEM((TAPS * SEGS, WIDTH), F32),
         pltpu.VMEM((256, WIDTH), BF16),
         pltpu.VMEM((256, WIDTH), BF16),
-        pltpu.VMEM((2, 2, ROWS, 256), BF16),
-        pltpu.VMEM((2, 2, ROWS, 256), BF16),
+        pltpu.VMEM((2, 2, ROWS // 2, WIDTH), BF16),
+        pltpu.VMEM((2, 2, ROWS // 2, WIDTH), BF16),
         pltpu.VMEM((2, 8, 2, WIDTH, 256), BF16),
         pltpu.VMEM((3, 4096, WIDTH), BF16),
-        pltpu.VMEM((2, 6, ROWS, 256), BF16),
-        pltpu.VMEM((2, 6, ROWS, 256), BF16),
+        pltpu.VMEM((2, 2, 6, ROWS // 2, 256), BF16),
+        pltpu.VMEM((2, 2, 6, ROWS // 2, 256), BF16),
         pltpu.VMEM((ROWS, WIDTH), F32),
         pltpu.VMEM((8, 4, 128, WIDTH), BF16),
-        pltpu.VMEM((ROWS, WIDTH), BF16),
+        pltpu.VMEM((ROWS, 2 * WIDTH), BF16),
         pltpu.VMEM((3, ROWS, WIDTH), F32),
         pltpu.VMEM((ROWS, LANES), F32),
         pltpu.VMEM((3, 16, WIDTH), BF16),
@@ -710,8 +757,8 @@
         dma((2, 8, 2)),
         dma((2, 2)),
         dma((2, 2)),
-        dma((2, 6)),
-        dma((2, 6)),
+        dma((2, 2, 6)),
+        dma((2, 2, 6)),
         dma((32,)),
         dma((8, 4)),
         dma((15,)),

time: 162 us -> 149 us (0.920)
  Pallas kernels: 158 us -> 146 us
    pallas_call x1, Pallas kernels: 158 us -> 146 us  [local(): pl.pallas_call(kernel, out_shape=jax.ShapeDtypeStruct((2, 256, WIDTH), BF...]
where the time goes in v2:
time: 149 us; the launch traced here: 148 us
  Pallas kernels  146 us (98%)
  local copies, waits for them, and re-layouts  1.87 us (1%)
    pallas_call x1, Pallas kernels, local(): pl.pallas_call(kernel, out_shape=jax.ShapeDtypeStruct((2, 256, WIDTH), BF...  146 us

profile of v2, /device:TPU:6, one launch (start us, length us, event | category | flops | bytes accessed | tf_op | source)
XLA Modules:
  0.0 148.4 jit_solution(10261377863773551456)
XLA Ops:
  0.0 146.5 %shard_map.127 = bf16[2,256,512]{2,1,0:T(8,128)(2,1)} custom-call(bf16[2,256,512]{2,1,0:T(8,128)(2,1)} %res_h.1, bf16[2,3,256,512]{3,2,1,0:T(8,128)(2,1)} %bitcast.6, f32[3,3,512]{2,1,0:T(4,128)} %sw1.1, bf16[128,512]{1,0:T(8,128)(2,1)} %filt.1, f32[1,512]{1,0:T(1,128)} %bitcast.8, bf16[512,256]{1,0:T(8,128)(2,1)} %wo1_h.1, f32[1,4096]{1,0:T(1,128)} %bitcast.7, ...), custom_call_target="tpu_custom_call" | custom-call | tf_op jit(solution)/shard_map/pallas_call | solution.py:767
  146.5 1.9 %copy.15 = bf16[2,256,512]{2,1,0:T(8,128)(2,1)} copy(bf16[2,256,512]{2,1,0:T(8,128)(2,1)} %shard_map.127) | data formatting | bytes 1048576

commit v3 on v2

--- a/solution.py
+++ b/solution.py
@@ -76,11 +76,13 @@
     holder = (y + xl) % 2 == 0
     relay = (y + xl) % 2 == 1
     ups = ((y + 1) % 4, (y + 3) % 4)
+    late_h = ((z + 2) % 4 // 2 + xh) % 2
+    odd = z % 2
 
     def place_of(k, row):
-        xs = (xl, 1 - xl, 1 - xl, xl)[k]
-        xhs = (xh, xh, 1 - xh, 1 - xh)[k]
-        return xs * 4 + xhs * 2 + row // 2
+        turn_h = (0, late_h, 1, 1 - late_h)[k]
+        turn_l = (0, 1, 1 - late_h, late_h)[k]
+        return (xl + turn_l) % 2 * 4 + (xh + turn_h) % 2 * 2 + row // 2
 
     def ctx_of(h, row):
         return (h * 4 + row) * 2 + core
@@ -159,10 +161,10 @@
                 for copy in reversed(copies):
                     copy.start()
 
-    def weight_last(stage):
+    def weight_late(stage, *ks):
         @pl.when(holder)
         def _():
-            for k in range(4):
+            for k in ks:
                 _, (index, copies), _, _ = weight_moves(stage, k)
                 weight_got(stage, index)
                 copies[0].start()
@@ -308,7 +310,7 @@
             pss.at[stage, part, i],
             prs.at[stage, part, i],
             c,
-            ztp(1 if i % 2 == 0 else 3, xl),
+            ztp(1 + 2 * (i % 2), xl),
         )
 
     def term(stage, part, d, half):
@@ -317,35 +319,43 @@
         weights = jnp.concatenate([w[stage, xl * 4 + dest, half], w[stage, (1 - xl) * 4 + dest, half]], axis=0)
         return jnp.dot(both, weights, preferred_element_type=F32)
 
-    def project_first(stage, part):
-        arrived(zn.at[stage, part], zr.at[stage, part])
-        for i, d, half in ((0, 2, 0), (1, 2, 1), (2, 1, 1), (3, 3, 0)):
-            if part == 0 and i in (0, 2, 3):
-                for source in range(2):
-                    weight_sibling(stage, source * 4 + (z + d) % 4)
+    early = ((0, 2, 0), (1, 2, 1), (3 - odd, 3 - 2 * odd, odd))
+    later = ((2 + odd, 1 + 2 * odd, 1 - odd),)
+    passed = ((5 - odd, 3 - 2 * odd, 1 - odd), (4 + odd, 1 + 2 * odd, odd))
+
+    def project_direct(stage, part, pieces):
+        for i, d, half in pieces:
             ps[stage, part, i] = term(stage, part, d, half).astype(BF16)
             p_copy(stage, part, i).start()
 
-    def project_own(stage, part):
-        if part == 0:
-            for source in range(2):
-                weight_sibling(stage, source * 4 + z)
-        for own in range(2):
-            pacc[HALF * part : HALF * (part + 1), 256 * own : 256 * (own + 1)] = term(stage, part, 0, own)
-
-    def project_relay(stage, part):
-        for i, d, half in ((4, 1, 0), (5, 3, 1)):
+    def project_relay(stage, part, pieces):
+        for i, d, half in pieces:
             mine = term(stage, part, d, half)
             arrived(pr.at[stage, part, i - 4], prs.at[stage, part, i - 4])
             ps[stage, part, i] = (mine + pr[stage, part, i - 4].astype(F32)).astype(BF16)
             p_copy(stage, part, i).start()
 
-    def project(stage):
-        project_first(stage, 0)
-        project_first(stage, 1)
-        project_relay(stage, 0)
+    def project_own(stage, part):
+        for own in range(2):
+            pacc[HALF * part : HALF * (part + 1), 256 * own : 256 * (own + 1)] = term(stage, part, 0, own)
+
+    def project_early(stage):
+        for d in (2, 3 - 2 * odd):
+            for source in range(2):
+                weight_sibling(stage, source * 4 + (z + d) % 4)
+        for part in range(2):
+            arrived(zn.at[stage, part], zr.at[stage, part])
+            project_direct(stage, part, early)
+
+    def project_rest(stage):
+        for d in (1 + 2 * odd, 0):
+            for source in range(2):
+                weight_sibling(stage, source * 4 + (z + d) % 4)
+        project_direct(stage, 0, later)
+        project_direct(stage, 1, later)
+        project_relay(stage, 0, passed)
         project_own(stage, 0)
-        project_relay(stage, 1)
+        project_relay(stage, 1, passed)
         project_own(stage, 1)
 
     def project_wait(stage, part):
@@ -401,13 +411,12 @@
     weight_relay(0, 1)
     filter_blocks(4)
     z_copy(0, 0).start()
+    weight_late(0, 0)
+    filter_blocks(8)
     weight_relay(0, 2)
-    filter_blocks(8)
+    weight_late(0, 1)
     filter_blocks(12)
     z_copy(0, 1).start()
-    weight_relay(0, 3)
-    weight_last(0)
-    weight_start(1, wo2_h)
 
     load_res.wait()
 
@@ -424,7 +433,12 @@
         for k in range(WIDTH // LANES):
             x32[1, k, rows(j), :] = x32[0, k, pl.ds(j, SEGS, stride=STEPS), :]
 
-    project(0)
+    weight_late(0, 2)
+    project_early(0)
+    weight_relay(0, 3)
+    weight_late(0, 3)
+    weight_start(1, wo2_h)
+    project_rest(0)
     weight_hold(1, 0, 1, 2)
     weight_relay(1, 0)
 
@@ -520,7 +534,7 @@
     absorb(xm, xp)
     have(xz, 0, 1, 2, 3)
     absorb(xz)
-    weight_last(1)
+    weight_late(1, 0, 1, 2, 3)
 
     def finish(i):
         here = pl.ds(i * 16 if isinstance(i, int) else pl.multiple_of(i * 16, 16), 16)
@@ -670,7 +684,8 @@
 
         z_copy(1, part).start()
 
-    project(1)
+    project_early(1)
+    project_rest(1)
     for part in range(2):
         project_wait(1, part)
 

time: 149 us -> 152 us (1.020)
  Pallas kernels: 146 us -> 149 us
    pallas_call x1, Pallas kernels: 146 us -> 149 us  [local(): pl.pallas_call(kernel, out_shape=jax.ShapeDtypeStruct((2, 256, WIDTH), BF...]
where the time goes in v3:
time: 152 us; the launch traced here: 151 us
  Pallas kernels  149 us (98%)
  local copies, waits for them, and re-layouts  1.87 us (1%)
    pallas_call x1, Pallas kernels, local(): pl.pallas_call(kernel, out_shape=jax.ShapeDtypeStruct((2, 256, WIDTH), BF...  149 us

profile of v3, /device:TPU:6, one launch (start us, length us, event | category | flops | bytes accessed | tf_op | source)
XLA Modules:
  0.0 151.3 jit_solution(17688149998933099946)
XLA Ops:
  0.0 149.4 %shard_map.127 = bf16[2,256,512]{2,1,0:T(8,128)(2,1)} custom-call(bf16[2,256,512]{2,1,0:T(8,128)(2,1)} %res_h.1, bf16[2,3,256,512]{3,2,1,0:T(8,128)(2,1)} %bitcast.6, f32[3,3,512]{2,1,0:T(4,128)} %sw1.1, bf16[128,512]{1,0:T(8,128)(2,1)} %filt.1, f32[1,512]{1,0:T(1,128)} %bitcast.8, bf16[512,256]{1,0:T(8,128)(2,1)} %wo1_h.1, f32[1,4096]{1,0:T(1,128)} %bitcast.7, ...), custom_call_target="tpu_custom_call" | custom-call | tf_op jit(solution)/shard_map/pallas_call | solution.py:782
  149.4 1.9 %copy.15 = bf16[2,256,512]{2,1,0:T(8,128)(2,1)} copy(bf16[2,256,512]{2,1,0:T(8,128)(2,1)} %shard_map.127) | data formatting | bytes 1048576

commit v4 on v2

--- a/solution.py
+++ b/solution.py
@@ -22,7 +22,7 @@
     res_h, qkv_h, sw1, filt, skip1, wo1_h, gain, win_h, sw2, rate, resid, skip2, wo2_h,
     out_h,
     qkv_v, xtail, x32, q32, uext, fb, pk_s, pk_r, zo, zn, w, win, ps, pr, pacc, mid, scaled, acc, ssq,
-    ltail_s, ltail, est, st_s, st_r, hin, obf, resv,
+    ltail_s, ltail, est, decays, weights, st_s, st_r, hin, obf, resv,
     loc, hs, hr, wsnd, fsnd, bsnd, wrecv, zs, zr, pss, prs, ags, agr, sts, strv,
 ):
     c = lax.axis_index("ctx")
@@ -119,6 +119,10 @@
         block = w.at[stage, index, core]
         return remote(block, block, sem, wrecv.at[stage, index, core], ctx, t)
 
+    def weight_pass_half(stage, index, half, sem, ctx):
+        block = w.at[stage, index, core, 256 * half : 256 * (half + 1), :]
+        return remote(block, block, sem, wrecv.at[stage, index, core], ctx, t)
+
     def weight_got(stage, index):
         arrived(w.at[stage, index, core], wrecv.at[stage, index, core])
 
@@ -132,12 +136,8 @@
         if k:
             held += [weight_pass(stage, here, fsnd.at[stage, n, k], ctx_of(xh, ups[n])) for n in range(2)]
         late = [sibling(far, 4 + k)]
-        below = [sibling(down, k)]
-        above = [sibling(up, 4 + k)]
-        if k % 2 == 0:
-            below.append(weight_pass(stage, down, fsnd.at[stage, 0, k], ctx_of(xh, ups[0])))
-        else:
-            above.append(weight_pass(stage, up, fsnd.at[stage, 0, k], ctx_of(xh, ups[1])))
+        below = [sibling(down, k), weight_pass_half(stage, down, 0, fsnd.at[stage, 0, k], ctx_of(xh, ups[0]))]
+        above = [sibling(up, 4 + k), weight_pass_half(stage, up, 1, fsnd.at[stage, 1, k], ctx_of(xh, ups[1]))]
         return (here, held), (far, late), (down, below), (up, above)
 
     def weight_hold(stage, *ks):
@@ -159,10 +159,10 @@
                 for copy in reversed(copies):
                     copy.start()
 
-    def weight_last(stage):
+    def weight_late(stage, *ks):
         @pl.when(holder)
         def _():
-            for k in range(4):
+            for k in ks:
                 _, (index, copies), _, _ = weight_moves(stage, k)
                 weight_got(stage, index)
                 copies[0].start()
@@ -265,7 +265,7 @@
 
     u_copy = remote(pk_s, pk_r, hs.at[1], hr.at[1], (c + 1) % 16, t)
     u_copy.start()
-    weight_hold(0, 0)
+    weight_hold(0, 0, 1, 2)
     weight_relay(0, 0)
 
     arrived(xtail, hr.at[0])
@@ -294,7 +294,6 @@
         uext[rows(2 * i), :] = jnp.where(seg % 4 < 2, pltpu.roll(got, 6, 0), pltpu.roll(even, 2, 0))
         uext[rows(1 + 2 * i), :] = jnp.where(seg % 4 < 2, got, pltpu.roll(odd, 2, 0))
 
-    weight_hold(0, 1, 2)
 
     HALF = ROWS // 2
 
@@ -366,7 +365,7 @@
         return own + jnp.concatenate([left, right], axis=1)
 
     def filter_blocks(first_block):
-        @pl.loop(first_block, first_block + 4)
+        @pl.loop(first_block, first_block + 2)
         def _(block):
             lane = lanes((block % 8) // 2)
             part = block // 8
@@ -397,16 +396,23 @@
                 ).astype(BF16)
 
     filter_blocks(0)
+    filter_blocks(2)
     weight_hold(0, 3)
     weight_relay(0, 1)
     filter_blocks(4)
+    filter_blocks(6)
     z_copy(0, 0).start()
+    weight_late(0, 0)
+    filter_blocks(8)
     weight_relay(0, 2)
-    filter_blocks(8)
+    weight_late(0, 1)
+    filter_blocks(10)
     filter_blocks(12)
+    weight_relay(0, 3)
+    weight_late(0, 2)
+    filter_blocks(14)
     z_copy(0, 1).start()
-    weight_relay(0, 3)
-    weight_last(0)
+    weight_late(0, 3)
     weight_start(1, wo2_h)
 
     load_res.wait()
@@ -520,7 +526,7 @@
     absorb(xm, xp)
     have(xz, 0, 1, 2, 3)
     absorb(xz)
-    weight_last(1)
+    weight_late(1, 0, 1, 2, 3)
 
     def finish(i):
         here = pl.ds(i * 16 if isinstance(i, int) else pl.multiple_of(i * 16, 16), 16)
@@ -574,13 +580,16 @@
         lane = lanes(lt)
         decay = [jnp.exp(-row_of(rate, n, lane)) for n in range(POLES)]
 
-        def step(j, states):
-            u = uext[rows(j), lane]
-            return tuple(decay[n] * states[n] + u for n in range(POLES))
-
-        states = lax.fori_loop(0, STEPS, step, tuple(jnp.zeros((SEGS, LANES), F32) for _ in range(POLES)))
+        def step(i, states):
+            for k in range(4):
+                u = uext[rows(4 * i + k), lane]
+                states = [decay[n] * states[n] + u for n in range(POLES)]
+            return tuple(states)
+
+        states = lax.fori_loop(0, STEPS // 4, step, tuple(jnp.zeros((SEGS, LANES), F32) for _ in range(POLES)))
         for n in range(POLES):
             est[rows(n), lane] = states[n]
+            decays[rows(n), lane] = decay[n]
 
     place = seg1 % 4
 
@@ -612,6 +621,12 @@
         def _(d=d):
             state_copy(d).start()
 
+    @pl.loop(0, WIDTH // LANES)
+    def _(lt):
+        lane = lanes(lt)
+        for n in range(POLES):
+            weights[rows(n), lane] = row_of(resid, n, lane) * jnp.sqrt(1.0 - jnp.exp(-2.0 * row_of(rate, n, lane)))
+
     packs = []
     for g in range(4):
         total = jnp.zeros((SEGS, WIDTH), F32)
@@ -635,11 +650,11 @@
             lane = lanes(lt)
             decay, weight, states = [], [], []
             for n in range(POLES):
-                r = row_of(rate, n, lane)
-                decay.append(jnp.exp(-r))
-                weight.append(row_of(resid, n, lane) * jnp.sqrt(1.0 - jnp.exp(-2.0 * r)))
+                decay.append(decays[rows(n), lane])
+                weight.append(weights[rows(n), lane])
                 state = est[rows(n), lane]
                 if part == 0:
+                    r = row_of(rate, n, lane)
                     k = (n // 4) * SEGS + n % 4
                     enter = jnp.where(
                         seg1 < 4,
@@ -742,6 +757,8 @@
         pltpu.VMEM((ROWS, LANES), F32),
         pltpu.VMEM((3, 16, WIDTH), BF16),
         pltpu.VMEM((3, 16, WIDTH), BF16),
+        pltpu.VMEM((POLES * SEGS, WIDTH), F32),
+        pltpu.VMEM((POLES * SEGS, WIDTH), F32),
         pltpu.VMEM((POLES * SEGS, WIDTH), F32),
         pltpu.VMEM((4 * SEGS, WIDTH), BF16),
         pltpu.VMEM((15, 4 * SEGS, WIDTH), BF16),

time: 149 us -> 143 us (0.960)
  Pallas kernels: 146 us -> 140 us
    pallas_call x1, Pallas kernels: 146 us -> 140 us  [local(): pl.pallas_call(kernel, out_shape=jax.ShapeDtypeStruct((2, 256, WIDTH), BF...]
where the time goes in v4:
time: 143 us; the launch traced here: 142 us
  Pallas kernels  140 us (98%)
  local copies, waits for them, and re-layouts  1.87 us (1%)
    pallas_call x1, Pallas kernels, local(): pl.pallas_call(kernel, out_shape=jax.ShapeDtypeStruct((2, 256, WIDTH), BF...  140 us

profile of v4, /device:TPU:6, one launch (start us, length us, event | category | flops | bytes accessed | tf_op | source)
XLA Modules:
  0.0 142.1 jit_solution(7510412574876599396)
XLA Ops:
  0.0 140.3 %shard_map.127 = bf16[2,256,512]{2,1,0:T(8,128)(2,1)} custom-call(bf16[2,256,512]{2,1,0:T(8,128)(2,1)} %res_h.1, bf16[2,3,256,512]{3,2,1,0:T(8,128)(2,1)} %bitcast.6, f32[3,3,512]{2,1,0:T(4,128)} %sw1.1, bf16[128,512]{1,0:T(8,128)(2,1)} %filt.1, f32[1,512]{1,0:T(1,128)} %bitcast.8, bf16[512,256]{1,0:T(8,128)(2,1)} %wo1_h.1, f32[1,4096]{1,0:T(1,128)} %bitcast.7, ...), custom_call_target="tpu_custom_call" | custom-call | tf_op jit(solution)/shard_map/pallas_call | solution.py:784
  140.3 1.9 %copy.15 = bf16[2,256,512]{2,1,0:T(8,128)(2,1)} copy(bf16[2,256,512]{2,1,0:T(8,128)(2,1)} %shard_map.127) | data formatting | bytes 1048576

commit v5 on v4

--- a/solution.py
+++ b/solution.py
@@ -339,13 +339,16 @@
             ps[stage, part, i] = (mine + pr[stage, part, i - 4].astype(F32)).astype(BF16)
             p_copy(stage, part, i).start()
 
-    def project(stage):
+    def project(stage, take, between):
         project_first(stage, 0)
+        project_own(stage, 0)
+        project_relay(stage, 0)
         project_first(stage, 1)
-        project_relay(stage, 0)
-        project_own(stage, 0)
+        project_own(stage, 1)
+        take(0)
         project_relay(stage, 1)
-        project_own(stage, 1)
+        between()
+        take(1)
 
     def project_wait(stage, part):
         for i in (2, 3, 4, 5):
@@ -430,10 +433,6 @@
         for k in range(WIDTH // LANES):
             x32[1, k, rows(j), :] = x32[0, k, pl.ds(j, SEGS, stride=STEPS), :]
 
-    project(0)
-    weight_hold(1, 0, 1, 2)
-    weight_relay(1, 0)
-
     sent = []
 
     def send(slot, quarter, tp):
@@ -446,11 +445,11 @@
 
     zp, zm, zz = ztp(1, xl), ztp(3, xl), ztp(2, xl)
     xp, xm, xz = ztp(1, 1 - xl), ztp(3, 1 - xl), ztp(2, 1 - xl)
-    for part in range(2):
+    def take_middle(part):
         project_wait(0, part)
 
         @pl.loop(0, 16)
-        def _(i, part=part):
+        def _(i):
             here = pl.ds(pl.multiple_of(part * HALF + i * 16, 16), 16)
             before = jnp.concatenate([x32[1, k, here, :] for k in range(WIDTH // LANES)], axis=1)
             value = (before + arrivals(0, part, i)).astype(BF16)
@@ -460,6 +459,12 @@
             send(t, quarter, xn)
             send(t, quarter, zp)
             send(t, quarter, zm)
+
+    def next_weights():
+        weight_hold(1, 0, 1, 2)
+        weight_relay(1, 0)
+
+    project(0, take_middle, next_weights)
 
     def have(slot, *quarters):
         for quarter in quarters:
@@ -528,47 +533,52 @@
     absorb(xz)
     weight_late(1, 0, 1, 2, 3)
 
-    def finish(i):
-        here = pl.ds(i * 16 if isinstance(i, int) else pl.multiple_of(i * 16, 16), 16)
+    def factors(start, count):
+        here = pl.ds(start if isinstance(start, int) else pl.multiple_of(start, count), count)
         meansq = jnp.sum(ssq[here, :], axis=1, keepdims=True) * (1.0 / 4096.0)
-        factor = lax.rsqrt(meansq + 1e-6)
-        values = [(acc[p, here, :] * factor).astype(BF16) for p in range(3)]
-        for p in range(3):
-            acc[p, here, :] = values[p].astype(F32)
-        return values
-
-    tails = finish(31)
+        ssq[here, :] = jnp.broadcast_to(lax.rsqrt(meansq + 1e-6), (count, LANES))
+
+    def rounded(p, here):
+        factor = jnp.concatenate([ssq[here, :]] * (WIDTH // LANES), axis=1)
+        return (acc[p, here, :] * factor).astype(BF16)
+
+    def normal(j):
+        return [rounded(p, rows(j)).astype(F32) for p in range(3)]
+
+    factors(ROWS - 16, 16)
     for p in range(3):
-        ltail_s[p] = tails[p]
+        ltail_s[p] = rounded(p, pl.ds(ROWS - 16, 16))
     l_copy = remote(ltail_s, ltail, hs.at[2], hr.at[2], (c + 1) % 16, t)
     l_copy.start()
 
-    @pl.loop(0, 31)
+    @pl.loop(0, 7)
     def _(i):
-        finish(i)
+        factors(i * 64, 64)
+
+    factors(448, 32)
+    factors(480, 16)
 
     def longer(j, now, before, before2):
         mixed = [tap(sw2, 0, p) * now[p] + tap(sw2, 1, p) * before[p] + tap(sw2, 2, p) * before2[p] for p in range(3)]
         q32[rows(j), :] = mixed[0]
         uext[rows(j), :] = mixed[1] * mixed[2]
 
-    @pl.loop(2, STEPS)
-    def _(j):
-        longer(
-            j,
-            [acc[p, rows(j), :] for p in range(3)],
-            [acc[p, rows(j - 1), :] for p in range(3)],
-            [acc[p, rows(j - 2), :] for p in range(3)],
-        )
+    y0, y1 = normal(0), normal(1)
+
+    def longer_step(j, carried):
+        now = normal(j)
+        before, before2 = carried
+        longer(j, now, before, before2)
+        return now, before
+
+    y63, y62 = lax.fori_loop(2, STEPS, longer_step, (y1, y0))
 
     arrived(ltail, hr.at[2])
     edge1, edge2 = [], []
     for p in range(3):
         got = ltail[p].astype(F32) * live
-        edge2.append(jnp.where(first, pltpu.roll(got[:SEGS], 5, 0), pltpu.roll(acc[p, rows(62), :], 1, 0)))
-        edge1.append(jnp.where(first, pltpu.roll(got[SEGS:], 5, 0), pltpu.roll(acc[p, rows(63), :], 1, 0)))
-    y0 = [acc[p, rows(0), :] for p in range(3)]
-    y1 = [acc[p, rows(1), :] for p in range(3)]
+        edge2.append(jnp.where(first, pltpu.roll(got[:SEGS], 5, 0), pltpu.roll(y62[p], 1, 0)))
+        edge1.append(jnp.where(first, pltpu.roll(got[SEGS:], 5, 0), pltpu.roll(y63[p], 1, 0)))
     longer(0, y0, edge1, edge2)
     longer(1, y1, y0, edge1)
 
@@ -685,12 +695,11 @@
 
         z_copy(1, part).start()
 
-    project(1)
-    for part in range(2):
+    def take_last(part):
         project_wait(1, part)
 
         @pl.loop(0, 16)
-        def _(i, part=part):
+        def _(i):
             base = mid[t, part * 2 + i // 8, pl.ds(pl.multiple_of((i % 8) * 16, 16), 16), :].astype(F32)
             value = base + arrivals(1, part, i)
             j = part * (STEPS // 2) + 2 * i
@@ -699,13 +708,14 @@
                 x32[2, k, pl.ds(j, SEGS, stride=STEPS), :] = piece[:SEGS]
                 x32[2, k, pl.ds(j + 1, SEGS, stride=STEPS), :] = piece[SEGS:]
 
-    @pl.loop(0, 32)
-    def _(i):
-        s = i // 16
-        r = (i % 16) * 16
-        here = pl.ds(pl.multiple_of(i * 16, 16), 16)
-        value = jnp.concatenate([x32[2, k, here, :] for k in range(WIDTH // LANES)], axis=1)
-        obf[s, pl.ds(pl.multiple_of(r, 16), 16), :] = value.astype(BF16)
+        @pl.loop(0, 8)
+        def _(i):
+            here = pl.ds(pl.multiple_of(i * STEPS + part * 32, 32), 32)
+            there = pl.ds(pl.multiple_of(i % 4 * STEPS + part * 32, 32), 32)
+            value = jnp.concatenate([x32[2, k, here, :] for k in range(WIDTH // LANES)], axis=1)
+            obf[i // 4, there, :] = value.astype(BF16)
+
+    project(1, take_last, lambda: None)
 
     store = pltpu.make_async_copy(obf, out_h, loc.at[3])
     store.start()

time: 143 us -> 146 us (1.021)
  Pallas kernels: 140 us -> 144 us
    pallas_call x1, Pallas kernels: 140 us -> 144 us  [local(): pl.pallas_call(kernel, out_shape=jax.ShapeDtypeStruct((2, 256, WIDTH), BF...]
where the time goes in v5:
time: 146 us
  Pallas kernels  144 us (99%)
  local copies, waits for them, and re-layouts  1.87 us (1%)
    pallas_call x1, Pallas kernels, local(): pl.pallas_call(kernel, out_shape=jax.ShapeDtypeStruct((2, 256, WIDTH), BF...  144 us

profile of v5, /device:TPU:6, one launch (start us, length us, event | category | flops | bytes accessed | tf_op | source)
XLA Modules:
  0.0 145.7 jit_solution(14640960588007651229)
XLA Ops:
  0.0 143.8 %shard_map.127 = bf16[2,256,512]{2,1,0:T(8,128)(2,1)} custom-call(bf16[2,256,512]{2,1,0:T(8,128)(2,1)} %res_h.1, bf16[2,3,256,512]{3,2,1,0:T(8,128)(2,1)} %bitcast.6, f32[3,3,512]{2,1,0:T(4,128)} %sw1.1, bf16[128,512]{1,0:T(8,128)(2,1)} %filt.1, f32[1,512]{1,0:T(1,128)} %bitcast.8, bf16[512,256]{1,0:T(8,128)(2,1)} %wo1_h.1, f32[1,4096]{1,0:T(1,128)} %bitcast.7, ...), custom_call_target="tpu_custom_call" | custom-call | tf_op jit(solution)/shard_map/pallas_call | solution.py:794
  143.8 1.9 %copy.15 = bf16[2,256,512]{2,1,0:T(8,128)(2,1)} copy(bf16[2,256,512]{2,1,0:T(8,128)(2,1)} %shard_map.127) | data formatting | bytes 1048576

commit v6 on v4

--- a/solution.py
+++ b/solution.py
@@ -21,7 +21,7 @@
 def kernel(
     res_h, qkv_h, sw1, filt, skip1, wo1_h, gain, win_h, sw2, rate, resid, skip2, wo2_h,
     out_h,
-    qkv_v, xtail, x32, q32, uext, fb, pk_s, pk_r, zo, zn, w, win, ps, pr, pacc, mid, scaled, acc, ssq,
+    qkv_v, xtail, x32, q32, uext, ueven, uodd, fb, pk_s, pk_r, zo, zn, w, win, ps, pr, pacc, mid, scaled, acc, ssq,
     ltail_s, ltail, est, decays, weights, st_s, st_r, hin, obf, resv,
     loc, hs, hr, wsnd, fsnd, bsnd, wrecv, zs, zr, pss, prs, ags, agr, sts, strv,
 ):
@@ -210,7 +210,9 @@
     def _(i):
         taps = filt[pl.ds(pl.multiple_of(i * 8, 8), 8), :].astype(F32)
         for k in range(8):
-            fb[rows(i * 8 + k), :] = jnp.broadcast_to(taps[k : k + 1, :], (SEGS, WIDTH))
+            fb[pl.ds(pl.multiple_of((i * 8 + k) * 16, 16), 16), :] = jnp.broadcast_to(
+                taps[k : k + 1, :], (16, WIDTH)
+            ).astype(BF16)
 
     load_qkv.wait()
     for s in range(2):
@@ -373,46 +375,54 @@
             j0 = part * 32 + r0
 
             def taps8(ib, totals):
-                base = 128 + j0 - 8 * ib - 7
-                window = uext[pl.ds(pl.multiple_of(base * SEGS, SEGS), 23 * SEGS), lane]
-                weights = fb[pl.ds(pl.multiple_of(ib * 64, 64), 64), lane]
+                base = 64 + j0 // 2 - 4 * ib - 3
+                window = pl.ds(pl.multiple_of(base * 16, 16), 11 * 16)
+                even, odd_ = ueven[window, lane], uodd[window, lane]
+                taps = fb[pl.ds(pl.multiple_of(ib * 128, 128), 128), lane]
                 totals = list(totals)
-                for b in range(8):
-                    f = weights[b * SEGS : (b + 1) * SEGS]
-                    for a in range(16):
-                        k = a + 7 - b
-                        totals[a] = totals[a] + f * window[k * SEGS : (k + 1) * SEGS]
+                for a in range(8):
+                    terms = []
+                    for b in range(8):
+                        k = 3 - b // 2 + a
+                        u = (odd_ if b % 2 else even)[k * 16 : (k + 1) * 16]
+                        terms.append(taps[b * 16 : (b + 1) * 16] * u)
+                    while len(terms) > 1:
+                        terms = [terms[n] + terms[n + 1] for n in range(0, len(terms), 2)]
+                    totals[a] = totals[a] + terms[0].astype(F32)
                 return tuple(totals)
 
-            totals = lax.fori_loop(0, 16, taps8, tuple(jnp.zeros((SEGS, LANES), F32) for _ in range(16)))
-            skip = jnp.broadcast_to(skip1[:, lane], (SEGS, LANES))
-            for a in range(0, 16, 2):
-                pair = []
-                for k in (a, a + 1):
-                    u = uext[rows(128 + j0 + k), lane]
-                    pair.append(q32[rows(j0 + k), lane] * (totals[k] + skip * u))
-                zo[0, part, pl.ds(pl.multiple_of((r0 + a) * SEGS, 16), 16), lane] = jnp.concatenate(
-                    pair, axis=0
-                ).astype(BF16)
-
+            totals = lax.fori_loop(0, 16, taps8, tuple(jnp.zeros((16, LANES), F32) for _ in range(8)))
+            skip = jnp.broadcast_to(skip1[:, lane], (16, LANES))
+            for a in range(8):
+                u = uext[rows(128 + j0 + 2 * a, 2), lane]
+                value = q32[rows(j0 + 2 * a, 2), lane] * (totals[a] + skip * u)
+                zo[0, part, pl.ds(pl.multiple_of((r0 + 2 * a) * SEGS, 16), 16), lane] = value.astype(BF16)
+
+    def pairs(first_pair, last_pair):
+        @pl.loop(first_pair, last_pair)
+        def _(i):
+            here = pl.ds(pl.multiple_of(i * 16, 16), 16)
+            ueven[here, :] = uext[rows(2 * i, 2), :].astype(BF16)
+            uodd[here, :] = uext[rows(2 * i - 1, 2), :].astype(BF16)
+
+    pairs(1, 96)
     filter_blocks(0)
     filter_blocks(2)
     weight_hold(0, 3)
-    weight_relay(0, 1)
     filter_blocks(4)
     filter_blocks(6)
     z_copy(0, 0).start()
+    filter_blocks(8)
+    filter_blocks(10)
+    weight_relay(0, 1)
+    filter_blocks(12)
+    filter_blocks(14)
+    z_copy(0, 1).start()
     weight_late(0, 0)
-    filter_blocks(8)
     weight_relay(0, 2)
     weight_late(0, 1)
-    filter_blocks(10)
-    filter_blocks(12)
     weight_relay(0, 3)
-    weight_late(0, 2)
-    filter_blocks(14)
-    z_copy(0, 1).start()
-    weight_late(0, 3)
+    weight_late(0, 2, 3)
     weight_start(1, wo2_h)
 
     load_res.wait()
@@ -741,7 +751,9 @@
         pltpu.VMEM((3, WIDTH // LANES, ROWS, LANES), F32),
         pltpu.VMEM((ROWS, WIDTH), F32),
         pltpu.VMEM((192 * SEGS, WIDTH), F32),
-        pltpu.VMEM((TAPS * SEGS, WIDTH), F32),
+        pltpu.VMEM((96 * 16, WIDTH), BF16),
+        pltpu.VMEM((96 * 16, WIDTH), BF16),
+        pltpu.VMEM((TAPS * 16, WIDTH), BF16),
         pltpu.VMEM((256, WIDTH), BF16),
         pltpu.VMEM((256, WIDTH), BF16),
         pltpu.VMEM((2, 2, ROWS // 2, WIDTH), BF16),

time: 143 us -> 144 us (level)
  no operation moved by 1% of the time
where the time goes in v6:
time: 144 us; the launch traced here: 142 us
  Pallas kernels  140 us (97%)
  local copies, waits for them, and re-layouts  1.87 us (1%)
    pallas_call x1, Pallas kernels, local(): pl.pallas_call(kernel, out_shape=jax.ShapeDtypeStruct((2, 256, WIDTH), BF...  140 us

profile of v6, /device:TPU:6, one launch (start us, length us, event | category | flops | bytes accessed | tf_op | source)
XLA Modules:
  0.0 141.7 jit_solution(10225129423704056228)
XLA Ops:
  0.0 139.8 %shard_map.127 = bf16[2,256,512]{2,1,0:T(8,128)(2,1)} custom-call(bf16[2,256,512]{2,1,0:T(8,128)(2,1)} %res_h.1, bf16[2,3,256,512]{3,2,1,0:T(8,128)(2,1)} %bitcast.6, f32[3,3,512]{2,1,0:T(4,128)} %sw1.1, bf16[128,512]{1,0:T(8,128)(2,1)} %filt.1, f32[1,512]{1,0:T(1,128)} %bitcast.8, bf16[512,256]{1,0:T(8,128)(2,1)} %wo1_h.1, f32[1,4096]{1,0:T(1,128)} %bitcast.7, ...), custom_call_target="tpu_custom_call" | custom-call | tf_op jit(solution)/shard_map/pallas_call | solution.py:796
  139.8 1.9 %copy.15 = bf16[2,256,512]{2,1,0:T(8,128)(2,1)} copy(bf16[2,256,512]{2,1,0:T(8,128)(2,1)} %shard_map.127) | data formatting | bytes 1048576

commit v7 on v6

--- a/solution.py
+++ b/solution.py
@@ -76,11 +76,13 @@
     holder = (y + xl) % 2 == 0
     relay = (y + xl) % 2 == 1
     ups = ((y + 1) % 4, (y + 3) % 4)
+    late_h = ((z + 2) % 4 // 2 + xh) % 2
+    odd = z % 2
 
     def place_of(k, row):
-        xs = (xl, 1 - xl, 1 - xl, xl)[k]
-        xhs = (xh, xh, 1 - xh, 1 - xh)[k]
-        return xs * 4 + xhs * 2 + row // 2
+        turn_h = (0, late_h, 1, 1 - late_h)[k]
+        turn_l = (0, 1, 1 - late_h, late_h)[k]
+        return (xl + turn_l) % 2 * 4 + (xh + turn_h) % 2 * 2 + row // 2
 
     def ctx_of(h, row):
         return (h * 4 + row) * 2 + core
@@ -267,7 +269,7 @@
 
     u_copy = remote(pk_s, pk_r, hs.at[1], hr.at[1], (c + 1) % 16, t)
     u_copy.start()
-    weight_hold(0, 0, 1, 2)
+    weight_hold(0, 0, 1)
     weight_relay(0, 0)
 
     arrived(xtail, hr.at[0])
@@ -309,7 +311,7 @@
             pss.at[stage, part, i],
             prs.at[stage, part, i],
             c,
-            ztp(1 if i % 2 == 0 else 3, xl),
+            ztp(1 + 2 * (i % 2), xl),
         )
 
     def term(stage, part, d, half):
@@ -318,35 +320,35 @@
         weights = jnp.concatenate([w[stage, xl * 4 + dest, half], w[stage, (1 - xl) * 4 + dest, half]], axis=0)
         return jnp.dot(both, weights, preferred_element_type=F32)
 
-    def project_first(stage, part):
-        arrived(zn.at[stage, part], zr.at[stage, part])
-        for i, d, half in ((0, 2, 0), (1, 2, 1), (2, 1, 1), (3, 3, 0)):
-            if part == 0 and i in (0, 2, 3):
-                for source in range(2):
-                    weight_sibling(stage, source * 4 + (z + d) % 4)
+    early = ((0, 2, 0), (1, 2, 1), (3 - odd, 3 - 2 * odd, odd))
+    later = ((2 + odd, 1 + 2 * odd, 1 - odd),)
+    passed = ((5 - odd, 3 - 2 * odd, 1 - odd), (4 + odd, 1 + 2 * odd, odd))
+
+    def project_direct(stage, part, pieces):
+        for i, d, half in pieces:
             ps[stage, part, i] = term(stage, part, d, half).astype(BF16)
             p_copy(stage, part, i).start()
 
-    def project_own(stage, part):
-        if part == 0:
-            for source in range(2):
-                weight_sibling(stage, source * 4 + z)
-        for own in range(2):
-            pacc[HALF * part : HALF * (part + 1), 256 * own : 256 * (own + 1)] = term(stage, part, 0, own)
-
-    def project_relay(stage, part):
-        for i, d, half in ((4, 1, 0), (5, 3, 1)):
+    def project_relay(stage, part, pieces):
+        for i, d, half in pieces:
             mine = term(stage, part, d, half)
             arrived(pr.at[stage, part, i - 4], prs.at[stage, part, i - 4])
             ps[stage, part, i] = (mine + pr[stage, part, i - 4].astype(F32)).astype(BF16)
             p_copy(stage, part, i).start()
 
-    def project(stage):
-        project_first(stage, 0)
-        project_first(stage, 1)
-        project_relay(stage, 0)
+    def project_own(stage, part):
+        for own in range(2):
+            pacc[HALF * part : HALF * (part + 1), 256 * own : 256 * (own + 1)] = term(stage, part, 0, own)
+
+    def project_weights(stage, *offsets):
+        for d in offsets:
+            for source in range(2):
+                weight_sibling(stage, source * 4 + (z + d) % 4)
+
+    def project_end(stage):
+        project_relay(stage, 0, passed)
         project_own(stage, 0)
-        project_relay(stage, 1)
+        project_relay(stage, 1, passed)
         project_own(stage, 1)
 
     def project_wait(stage, part):
@@ -406,12 +408,10 @@
             uodd[here, :] = uext[rows(2 * i - 1, 2), :].astype(BF16)
 
     pairs(1, 96)
-    filter_blocks(0)
-    filter_blocks(2)
-    weight_hold(0, 3)
-    filter_blocks(4)
-    filter_blocks(6)
+    for first_block in range(0, 8, 2):
+        filter_blocks(first_block)
     z_copy(0, 0).start()
+    weight_hold(0, 2, 3)
     filter_blocks(8)
     filter_blocks(10)
     weight_relay(0, 1)
@@ -419,11 +419,6 @@
     filter_blocks(14)
     z_copy(0, 1).start()
     weight_late(0, 0)
-    weight_relay(0, 2)
-    weight_late(0, 1)
-    weight_relay(0, 3)
-    weight_late(0, 2, 3)
-    weight_start(1, wo2_h)
 
     load_res.wait()
 
@@ -440,7 +435,20 @@
         for k in range(WIDTH // LANES):
             x32[1, k, rows(j), :] = x32[0, k, pl.ds(j, SEGS, stride=STEPS), :]
 
-    project(0)
+    weight_relay(0, 2)
+    weight_late(0, 1, 2)
+    project_weights(0, 2, 3 - 2 * odd)
+    arrived(zn.at[0, 0], zr.at[0, 0])
+    project_direct(0, 0, early)
+    weight_relay(0, 3)
+    arrived(zn.at[0, 1], zr.at[0, 1])
+    project_direct(0, 1, early)
+    weight_late(0, 3)
+    weight_start(1, wo2_h)
+    project_weights(0, 1 + 2 * odd, 0)
+    project_direct(0, 0, later)
+    project_direct(0, 1, later)
+    project_end(0)
     weight_hold(1, 0, 1, 2)
     weight_relay(1, 0)
 
@@ -695,7 +703,11 @@
 
         z_copy(1, part).start()
 
-    project(1)
+    project_weights(1, 0, 1, 2, 3)
+    for part in range(2):
+        arrived(zn.at[1, part], zr.at[1, part])
+        project_direct(1, part, early + later)
+    project_end(1)
     for part in range(2):
         project_wait(1, part)
 

time: 144 us -> 147 us (1.021); the launches traced: 142 us -> 147 us
  Pallas kernels: 140 us -> 145 us
    pallas_call x1, Pallas kernels: 140 us -> 145 us  [local(): pl.pallas_call(kernel, out_shape=jax.ShapeDtypeStruct((2, 256, WIDTH), BF...]
where the time goes in v7:
time: 147 us
  Pallas kernels  145 us (99%)
  local copies, waits for them, and re-layouts  1.87 us (1%)
    pallas_call x1, Pallas kernels, local(): pl.pallas_call(kernel, out_shape=jax.ShapeDtypeStruct((2, 256, WIDTH), BF...  145 us

profile of v7, /device:TPU:6, one launch (start us, length us, event | category | flops | bytes accessed | tf_op | source)
XLA Modules:
  0.0 146.8 jit_solution(10592565954861662573)
XLA Ops:
  0.0 144.9 %shard_map.127 = bf16[2,256,512]{2,1,0:T(8,128)(2,1)} custom-call(bf16[2,256,512]{2,1,0:T(8,128)(2,1)} %res_h.1, bf16[2,3,256,512]{3,2,1,0:T(8,128)(2,1)} %bitcast.6, f32[3,3,512]{2,1,0:T(4,128)} %sw1.1, bf16[128,512]{1,0:T(8,128)(2,1)} %filt.1, f32[1,512]{1,0:T(1,128)} %bitcast.8, bf16[512,256]{1,0:T(8,128)(2,1)} %wo1_h.1, f32[1,4096]{1,0:T(1,128)} %bitcast.7, ...), custom_call_target="tpu_custom_call" | custom-call | tf_op jit(solution)/shard_map/pallas_call | solution.py:808
  144.9 1.9 %copy.15 = bf16[2,256,512]{2,1,0:T(8,128)(2,1)} copy(bf16[2,256,512]{2,1,0:T(8,128)(2,1)} %shard_map.127) | data formatting | bytes 1048576

commit v8 on v4

--- a/solution.py
+++ b/solution.py
@@ -493,59 +493,72 @@
             acc[i // 2, :, cols] = product if fresh else acc[i // 2, :, cols] + product
 
     absorb(t, fresh=True)
-    weight_hold(1, 3)
-    weight_relay(1, 1)
+    have(zm, 2, 3)
+    send(zm, 2, xn)
+    send(zm, 3, xn)
+    send(zm, 2, zp)
+    have(zp, 2, 3)
+    send(zp, 2, xn)
+    send(zp, 3, xn)
+    send(zp, 3, zm)
     have(xn, 0, 1)
     for quarter in range(2):
         send(xn, quarter, zp)
         send(xn, quarter, zm)
-    have(zm, 0, 1, 2, 3)
+    have(zm, 0, 1)
     send(zm, 0, zp)
-    send(zm, 2, zp)
-    send(zm, 2, xn)
-    send(zm, 3, xn)
-    have(zp, 0, 1, 2, 3)
+    have(zp, 0, 1)
     send(zp, 1, zm)
-    send(zp, 3, zm)
-    send(zp, 2, xn)
-    send(zp, 3, xn)
+    weight_hold(1, 3)
     absorb(zm, zp)
-    weight_relay(1, 2)
+    have(zz, 2, 3)
+    send(zz, 2, xn)
+    send(zz, 3, xn)
     have(xm, 0, 1)
     send(xm, 0, zp)
     have(xp, 0, 1)
     send(xp, 1, zm)
-    have(zz, 0, 1, 2, 3)
-    send(zz, 2, xn)
-    send(zz, 3, xn)
+    weight_relay(1, 1)
+    have(zz, 0, 1)
     have(xn, 2, 3)
     absorb(xn, zz)
-    weight_relay(1, 3)
+    weight_relay(1, 2)
     have(xm, 2, 3)
     have(xp, 2, 3)
     absorb(xm, xp)
+    weight_relay(1, 3)
     have(xz, 0, 1, 2, 3)
     absorb(xz)
-    weight_late(1, 0, 1, 2, 3)
+
+    def factors(start, count):
+        here = pl.ds(start if isinstance(start, int) else pl.multiple_of(start, 64), count)
+        meansq = jnp.sum(ssq[here, :], axis=1, keepdims=True) * (1.0 / 4096.0)
+        ssq[here, :] = jnp.broadcast_to(lax.rsqrt(meansq + 1e-6), (count, LANES))
 
     def finish(i):
         here = pl.ds(i * 16 if isinstance(i, int) else pl.multiple_of(i * 16, 16), 16)
-        meansq = jnp.sum(ssq[here, :], axis=1, keepdims=True) * (1.0 / 4096.0)
-        factor = lax.rsqrt(meansq + 1e-6)
+        factor = jnp.concatenate([ssq[here, :]] * (WIDTH // LANES), axis=1)
         values = [(acc[p, here, :] * factor).astype(BF16) for p in range(3)]
         for p in range(3):
             acc[p, here, :] = values[p].astype(F32)
         return values
 
+    factors(448, 64)
     tails = finish(31)
     for p in range(3):
         ltail_s[p] = tails[p]
     l_copy = remote(ltail_s, ltail, hs.at[2], hr.at[2], (c + 1) % 16, t)
     l_copy.start()
 
+    @pl.loop(0, 7)
+    def _(i):
+        factors(i * 64, 64)
+
     @pl.loop(0, 31)
     def _(i):
         finish(i)
+
+    weight_late(1, 0, 1, 2, 3)
 
     def longer(j, now, before, before2):
         mixed = [tap(sw2, 0, p) * now[p] + tap(sw2, 1, p) * before[p] + tap(sw2, 2, p) * before2[p] for p in range(3)]

time: 143 us -> 143 us (level)
  no operation moved by 1% of the time
where the time goes in v8:
time: 143 us
  Pallas kernels  141 us (99%)
  local copies, waits for them, and re-layouts  1.87 us (1%)
    pallas_call x1, Pallas kernels, local(): pl.pallas_call(kernel, out_shape=jax.ShapeDtypeStruct((2, 256, WIDTH), BF...  141 us

profile of v8, /device:TPU:6, one launch (start us, length us, event | category | flops | bytes accessed | tf_op | source)
XLA Modules:
  0.0 143.0 jit_solution(9359318357921620715)
XLA Ops:
  0.0 141.1 %shard_map.127 = bf16[2,256,512]{2,1,0:T(8,128)(2,1)} custom-call(bf16[2,256,512]{2,1,0:T(8,128)(2,1)} %res_h.1, bf16[2,3,256,512]{3,2,1,0:T(8,128)(2,1)} %bitcast.6, f32[3,3,512]{2,1,0:T(4,128)} %sw1.1, bf16[128,512]{1,0:T(8,128)(2,1)} %filt.1, f32[1,512]{1,0:T(1,128)} %bitcast.8, bf16[512,256]{1,0:T(8,128)(2,1)} %wo1_h.1, f32[1,4096]{1,0:T(1,128)} %bitcast.7, ...), custom_call_target="tpu_custom_call" | custom-call | tf_op jit(solution)/shard_map/pallas_call | solution.py:797
  141.1 1.9 %copy.15 = bf16[2,256,512]{2,1,0:T(8,128)(2,1)} copy(bf16[2,256,512]{2,1,0:T(8,128)(2,1)} %shard_map.127) | data formatting | bytes 1048576

commit v9 on v4

--- a/solution.py
+++ b/solution.py
@@ -666,19 +666,19 @@
             skip = jnp.broadcast_to(skip2[:, lane], (SEGS, LANES))
 
             def step(i, states):
-                pair = []
-                for k in range(2):
-                    j = part * (STEPS // 2) + 2 * i + k
+                values = []
+                for k in range(4):
+                    j = part * (STEPS // 2) + 4 * i + k
                     u = uext[rows(j), lane]
                     states = [decay[n] * states[n] + u for n in range(POLES)]
                     terms = [weight[n] * states[n] for n in range(POLES)]
                     while len(terms) > 1:
                         terms = [terms[a] + terms[a + 1] for a in range(0, len(terms), 2)]
-                    pair.append(q32[rows(j), lane] * (terms[0] + skip * u))
-                zo[1, part, pl.ds(pl.multiple_of(i * 16, 16), 16), lane] = jnp.concatenate(pair, axis=0).astype(BF16)
+                    values.append(q32[rows(j), lane] * (terms[0] + skip * u))
+                zo[1, part, pl.ds(pl.multiple_of(i * 32, 32), 32), lane] = jnp.concatenate(values, axis=0).astype(BF16)
                 return tuple(states)
 
-            states = lax.fori_loop(0, STEPS // 4, step, tuple(states))
+            states = lax.fori_loop(0, STEPS // 8, step, tuple(states))
             if part == 0:
                 for n in range(POLES):
                     est[rows(n), lane] = states[n]
@@ -699,13 +699,12 @@
                 x32[2, k, pl.ds(j, SEGS, stride=STEPS), :] = piece[:SEGS]
                 x32[2, k, pl.ds(j + 1, SEGS, stride=STEPS), :] = piece[SEGS:]
 
-    @pl.loop(0, 32)
-    def _(i):
-        s = i // 16
-        r = (i % 16) * 16
-        here = pl.ds(pl.multiple_of(i * 16, 16), 16)
-        value = jnp.concatenate([x32[2, k, here, :] for k in range(WIDTH // LANES)], axis=1)
-        obf[s, pl.ds(pl.multiple_of(r, 16), 16), :] = value.astype(BF16)
+        @pl.loop(0, 8)
+        def _(i, part=part):
+            here = pl.ds(pl.multiple_of(i * STEPS + part * 32, 32), 32)
+            there = pl.ds(pl.multiple_of(i % 4 * STEPS + part * 32, 32), 32)
+            value = jnp.concatenate([x32[2, k, here, :] for k in range(WIDTH // LANES)], axis=1)
+            obf[i // 4, there, :] = value.astype(BF16)
 
     store = pltpu.make_async_copy(obf, out_h, loc.at[3])
     store.start()

time: 143 us -> 142 us (level)
  no operation moved by 1% of the time
where the time goes in v9:
time: 142 us
  Pallas kernels  140 us (99%)
  local copies, waits for them, and re-layouts  1.87 us (1%)
    pallas_call x1, Pallas kernels, local(): pl.pallas_call(kernel, out_shape=jax.ShapeDtypeStruct((2, 256, WIDTH), BF...  140 us

profile of v9, /device:TPU:6, one launch (start us, length us, event | category | flops | bytes accessed | tf_op | source)
XLA Modules:
  0.0 141.7 jit_solution(5653142027212713436)
XLA Ops:
  0.0 139.8 %shard_map.127 = bf16[2,256,512]{2,1,0:T(8,128)(2,1)} custom-call(bf16[2,256,512]{2,1,0:T(8,128)(2,1)} %res_h.1, bf16[2,3,256,512]{3,2,1,0:T(8,128)(2,1)} %bitcast.6, f32[3,3,512]{2,1,0:T(4,128)} %sw1.1, bf16[128,512]{1,0:T(8,128)(2,1)} %filt.1, f32[1,512]{1,0:T(1,128)} %bitcast.8, bf16[512,256]{1,0:T(8,128)(2,1)} %wo1_h.1, f32[1,4096]{1,0:T(1,128)} %bitcast.7, ...), custom_call_target="tpu_custom_call" | custom-call | tf_op jit(solution)/shard_map/pallas_call | solution.py:783
  139.8 1.9 %copy.15 = bf16[2,256,512]{2,1,0:T(8,128)(2,1)} copy(bf16[2,256,512]{2,1,0:T(8,128)(2,1)} %shard_map.127) | data formatting | bytes 1048576

commit v10 on v9

--- a/solution.py
+++ b/solution.py
@@ -408,11 +408,10 @@
     weight_late(0, 1)
     filter_blocks(10)
     filter_blocks(12)
-    weight_relay(0, 3)
-    weight_late(0, 2)
     filter_blocks(14)
     z_copy(0, 1).start()
-    weight_late(0, 3)
+    weight_relay(0, 3)
+    weight_late(0, 2, 3)
     weight_start(1, wo2_h)
 
     load_res.wait()

time: 142 us -> 143 us (level)
  no operation moved by 1% of the time
where the time goes in v10:
time: 143 us; the launch traced here: 142 us
  Pallas kernels  140 us (98%)
  local copies, waits for them, and re-layouts  1.87 us (1%)
    pallas_call x1, Pallas kernels, local(): pl.pallas_call(kernel, out_shape=jax.ShapeDtypeStruct((2, 256, WIDTH), BF...  140 us

profile of v10, /device:TPU:6, one launch (start us, length us, event | category | flops | bytes accessed | tf_op | source)
XLA Modules:
  0.0 142.1 jit_solution(2458656664415453548)
XLA Ops:
  0.0 140.2 %shard_map.127 = bf16[2,256,512]{2,1,0:T(8,128)(2,1)} custom-call(bf16[2,256,512]{2,1,0:T(8,128)(2,1)} %res_h.1, bf16[2,3,256,512]{3,2,1,0:T(8,128)(2,1)} %bitcast.6, f32[3,3,512]{2,1,0:T(4,128)} %sw1.1, bf16[128,512]{1,0:T(8,128)(2,1)} %filt.1, f32[1,512]{1,0:T(1,128)} %bitcast.8, bf16[512,256]{1,0:T(8,128)(2,1)} %wo1_h.1, f32[1,4096]{1,0:T(1,128)} %bitcast.7, ...), custom_call_target="tpu_custom_call" | custom-call | tf_op jit(solution)/shard_map/pallas_call | solution.py:782
  140.2 1.9 %copy.15 = bf16[2,256,512]{2,1,0:T(8,128)(2,1)} copy(bf16[2,256,512]{2,1,0:T(8,128)(2,1)} %shard_map.127) | data formatting | bytes 1048576
